TPU v7x, 32 devices: a whole 2x2x4 slice. The times are simulated.
32 devices in a mesh: tile: 8 (over z, y), attr: 4 (over x, core).
Axes of the slice: x: 2, y: 2, z: 4, core: 2. Of those that a mesh axis runs over, the one named last changes fastest.
Arguments:
- geometry: float32 [6, 65536], P(None, 'tile'), as said below
- sh_coeffs: float32 [48, 65536], P('attr', 'tile'), may hold values from -3 to 3
- view_angles: float32 [2, 65536], P(None, 'tile'), may hold values from -3.140625 to 3.140625
- visible: int32 [64, 16], P(('tile', 'attr')), may hold values from 0 to 255, as said below
- counts: int32 [64], P(('tile', 'attr')), may hold values from 1 to 16, as said below
- order: int32 [64, 16], P(('tile', 'attr')), may hold values from 0 to 15, each once within a row
- image_cot: float32 [64, 3, 256], P(('tile', 'attr')), may hold values from -6 to 6
Outputs:
- picture: float32 [64, 3, 256], P(('tile', 'attr'))
- grad_geometry: float32 [6, 65536], P(None, 'tile')
- grad_sh: float32 [48, 65536], P('attr', 'tile')
Inputs may be any that keep to these rules, and one draw needn't show every extreme that they name: `visible`: each tile lists 16 distinct block ids. Tile i and tile i + 1 of one device list the same blocks. The tiles of one device name at most 2 distinct blocks of one owner (id // 32), and exactly that many of some owner. The first counts[t] entries of tile t's depth order are live. `order`: A permutation of the list positions of the tile. `geometry`: row 0 and 1 between -4 and 20, rows 2 and 3 the logarithms of 0.1 * 16 to 0.25 * 16, row 4 an angle, row 5 within 5 below log(100 / 4096).
All inputs are finite; a program needn't handle non-finite values.
Results may differ from a plain program's by a relative error of at most 0.0003.
Values sent between devices are 32-bit elements; how exact they have to be, the bound alone decides.
A program may use at most 64 MiB of HBM per device.

v0:
```python
import functools
import jax
import jax.numpy as jnp
from jax import lax
from jax.experimental import pallas as pl
from jax.experimental.pallas import tpu as pltpu
from jax.sharding import PartitionSpec as P

BLOCK = 256
SIDE = 16
PIX = SIDE * SIDE
MID = 0.5 * SIDE
LOG2E = 1.4426950408889634
LN2 = 0.6931471805599453


band_zero = 0.28209479177387814
band_one = 0.4886025119029199
band_two = (
    1.0925484305920792,
    -1.0925484305920792,
    0.31539156525252005,
    -1.0925484305920792,
    0.5462742152960396,
)
band_three = (
    -0.5900435899266435,
    2.890611442640554,
    -0.4570457994644658,
    0.3731763325901154,
    -0.4570457994644658,
    1.445305721320277,
    -0.5900435899266435,
)


def sh_basis(view_angles):
    azimuth = view_angles[0]
    elevation = view_angles[1]
    dir_x = jnp.cos(azimuth) * jnp.cos(elevation)
    dir_y = jnp.sin(azimuth) * jnp.cos(elevation)
    dir_z = jnp.sin(elevation)
    sq_x = dir_x * dir_x
    sq_y = dir_y * dir_y
    sq_z = dir_z * dir_z
    basis_rows = [
        band_zero * jnp.ones_like(dir_x),
        -band_one * dir_y,
        band_one * dir_z,
        -band_one * dir_x,
        band_two[0] * dir_x * dir_y,
        band_two[1] * dir_y * dir_z,
        band_two[2] * (2.0 * sq_z - sq_x - sq_y),
        band_two[3] * dir_x * dir_z,
        band_two[4] * (sq_x - sq_y),
        band_three[0] * dir_y * (3.0 * sq_x - sq_y),
        band_three[1] * dir_x * dir_y * dir_z,
        band_three[2] * dir_y * (4.0 * sq_z - sq_x - sq_y),
        band_three[3] * dir_z * (2.0 * sq_z - 3.0 * sq_x - 3.0 * sq_y),
        band_three[4] * dir_x * (4.0 * sq_z - sq_x - sq_y),
        band_three[5] * dir_z * (sq_x - sq_y),
        band_three[6] * dir_x * (sq_x - 3.0 * sq_y),
    ]
    return basis_rows


def split2(x):
    high = x.astype(jnp.bfloat16)
    low = (x - high.astype(jnp.float32)).astype(jnp.bfloat16)
    return jnp.concatenate([high, low], axis=1)


def dot(a, b):
    return jnp.dot(a, b, preferred_element_type=jnp.float32)


def blend_kernel(tiles, seq_ref, counts_ref, held_ref, cot_rows_ref, cot_cols_ref, pic_ref, grad_ref, part_ref, ratio_ref):
    f32, bf16 = jnp.float32, jnp.bfloat16
    row = lax.broadcasted_iota(jnp.int32, (2 * BLOCK, BLOCK), 0)
    row = jnp.where(row >= BLOCK, row - BLOCK, row)
    col = lax.broadcasted_iota(jnp.int32, (2 * BLOCK, BLOCK), 1)
    before = jnp.where(row < col, -1.0, 0.0).astype(bf16)
    upto = jnp.where(row <= col, 1.0, 0.0).astype(bf16)

    def monomials(shape, dim, width):
        pixel = lax.broadcasted_iota(jnp.int32, shape, dim)
        kind = lax.broadcasted_iota(jnp.int32, shape, 1 - dim) & (width - 1)
        x = (pixel & (SIDE - 1)).astype(f32) + (0.5 - MID)
        y = (pixel // SIDE).astype(f32) + (0.5 - MID)
        out = jnp.where(kind == 0, 1.0, 0.0)
        for k, value in ((1, x), (2, y), (3, x * x), (4, x * y), (5, y * y)):
            out = jnp.where(kind == k, value, out)
        return out.astype(bf16)

    mono_cols = monomials((PIX, 48), 0, 16)
    mono_rows = monomials((8, PIX), 1, 8)
    cot_lhs, cot_rows = [], []
    for t in range(tiles):
        g = cot_cols_ref[t]
        high = g.astype(bf16).astype(f32)
        lane = lax.broadcasted_iota(jnp.int32, g.shape, 1)
        cot_lhs.append(jnp.where(lane < 48, high, g - high).astype(bf16))
        g = cot_rows_ref[t]
        high = g.astype(bf16).astype(f32)
        cot_rows.append(jnp.concatenate([high, g - high], axis=0).astype(bf16))

    grad_ref[...] = jnp.zeros_like(grad_ref)
    lives = [counts_ref[t] for t in range(tiles)]
    longest = functools.reduce(jnp.maximum, lives)

    lhs = []
    for t in range(tiles):
        wide = jnp.concatenate([mono_cols.astype(f32), jnp.zeros((PIX, 48), f32)], axis=1)
        lhs.append(jnp.concatenate([wide.astype(bf16), cot_lhs[t]], axis=0))
    head = lax.broadcasted_iota(jnp.int32, (16, BLOCK), 0) == 0

    def forward(j, carry):
        keep_before, sum_before, pictures = carry
        alphas, values, losses, helds, spots = [], [], [], [], []
        for t in range(tiles):
            at = seq_ref[t, j]
            hidden = jnp.where(j < lives[t], 0.0, -16384.0)
            held = held_ref[at]
            parts = split3(jnp.where(head, held + hidden, held))
            rows = jnp.concatenate(parts, axis=0)
            both = dot(lhs[t], jnp.concatenate([rows, rows], axis=0))
            alpha = jnp.exp2(both[:PIX])
            alphas.append(alpha)
            values.append(both[PIX:])
            losses.append(jnp.log(1.0 - alpha) * -LOG2E)
            helds.append(jnp.concatenate(parts[:2], axis=0))
            spots.append(at)
        loss = jnp.concatenate(losses, axis=0)
        keep_in = dot(split2(loss), before) + keep_before
        keep_before = keep_in[:, BLOCK - 1 :] - loss[:, BLOCK - 1 :]
        alpha = jnp.concatenate(alphas, axis=0)
        weight = alpha * jnp.exp2(keep_in)
        value = weight * jnp.concatenate(values, axis=0)
        total = dot(split2(value), upto) + sum_before
        sum_before = total[:, BLOCK - 1 :]
        ratio = alpha * jnp.exp2(loss)
        part_ref[j] = value + ratio * total
        ratio_ref[j] = ratio
        w2 = split2(weight)
        shown = []
        for t in range(tiles):
            w_high, w_low = w2[t * PIX : (t + 1) * PIX, :BLOCK], w2[t * PIX : (t + 1) * PIX, BLOCK:]
            rows = lax.dot_general(helds[t], w_high, (((1,), (1,)), ((), ())), preferred_element_type=f32)
            rows = rows + lax.dot_general(helds[t], w_low, (((1,), (1,)), ((), ())), preferred_element_type=f32)
            shown.append(pictures[t] + rows[:16] + rows[16:])
            colour_grad = dot(cot_rows[t], w_high) + dot(cot_rows[t], w_low)
            grad_ref[spots[t], 0:8, :] += colour_grad[:8] + colour_grad[8:]
        return keep_before, sum_before, tuple(shown)

    zero = jnp.zeros((tiles * PIX, 1), f32)
    start = (zero, zero, tuple(jnp.zeros((16, PIX), f32) for _ in range(tiles)))
    _, ends, pictures = lax.fori_loop(0, longest, forward, start)
    for t in range(tiles):
        pic_ref[t] = pictures[t]

    def backward(j, _):
        for t in range(tiles):
            pixels = slice(t * PIX, (t + 1) * PIX)
            d2 = split2(part_ref[j, pixels] - ratio_ref[j, pixels] * ends[pixels])
            moments = dot(mono_rows, d2[:, :BLOCK]) + dot(mono_rows, d2[:, BLOCK:])
            grad_ref[seq_ref[t, j], 8:16, :] += moments
        return 0

    lax.fori_loop(0, longest, backward, 0)


def blend(seq, counts, held, image_cot):
    tiles = image_cot.shape[0]
    rows = held.shape[0]
    cot_rows = jnp.pad(image_cot, ((0, 0), (0, 5), (0, 0)))
    cot_cols = jnp.pad(jnp.swapaxes(image_cot, 1, 2), ((0, 0), (0, 0), (6, 7)))
    cot_cols = jnp.tile(cot_cols, (1, 1, 6))
    smem = pl.BlockSpec(memory_space=pltpu.SMEM)
    vmem = pl.BlockSpec(memory_space=pltpu.VMEM)
    picture, grads = pl.pallas_call(
        functools.partial(blend_kernel, tiles),
        name="blend",
        out_shape=(
            jax.ShapeDtypeStruct((tiles, 16, PIX), jnp.float32),
            jax.ShapeDtypeStruct((rows, 16, BLOCK), jnp.float32),
        ),
        in_specs=[smem, smem, vmem, vmem, vmem],
        out_specs=(vmem, vmem),
        scratch_shapes=[
            pltpu.VMEM((seq.shape[1], tiles * PIX, BLOCK), jnp.float32),
            pltpu.VMEM((seq.shape[1], tiles * PIX, BLOCK), jnp.float32),
        ],
        compiler_params=pltpu.CompilerParams(vmem_limit_bytes=28 * 1024 * 1024),
    )(seq, counts, held, cot_rows, cot_cols)
    return picture[:, 6:9], grads


def splat_terms(geometry):
    mx, my = geometry[0] - MID, geometry[1] - MID
    c, s = jnp.cos(geometry[4]), jnp.sin(geometry[4])
    e1, e2 = jnp.exp(-2.0 * geometry[2]), jnp.exp(-2.0 * geometry[3])
    cc, ss, cs = c * c, s * s, c * s
    a = cc * e1 + ss * e2
    b = cs * (e1 - e2)
    d = ss * e1 + cc * e2
    return mx, my, e1, e2, cc, ss, cs, a, b, d, geometry[5]


def exponent_rows(terms):
    mx, my, e1, e2, cc, ss, cs, a, b, d, logit = terms
    bx, by = a * mx + b * my, b * mx + d * my
    log_opacity = jnp.minimum(logit, 0.0) - jnp.log1p(jnp.exp(-jnp.abs(logit)))
    one = log_opacity - 0.5 * (mx * bx + my * by)
    return [LOG2E * r for r in (one, bx, by, -0.5 * a, -b, -0.5 * d)]


def geometry_grads(terms, m):
    mx, my, e1, e2, cc, ss, cs, a, b, d, logit = terms
    n0 = m[0]
    nx, ny = m[1] - mx * n0, m[2] - my * n0
    nxx = m[3] - mx * (m[1] + nx)
    nxy = m[4] - mx * m[2] - my * nx
    nyy = m[5] - my * (m[2] + ny)
    return [
        a * nx + b * ny,
        b * nx + d * ny,
        e1 * (cc * nxx + 2.0 * cs * nxy + ss * nyy),
        e2 * (ss * nxx - 2.0 * cs * nxy + cc * nyy),
        (e2 - e1) * (cs * (nyy - nxx) + (cc - ss) * nxy),
        n0 / (1.0 + jnp.exp(logit)),
    ]


MESH = pl.DeviceIdType.MESH


def greet(peers):
    barrier = pltpu.get_barrier_semaphore()
    tile, attr, owners, extra = peers

    def hello(step, _):
        other = (tile + step) % owners
        pl.semaphore_signal(barrier, inc=1, device_id=(other, attr), device_id_type=MESH)
        return 0

    lax.fori_loop(1, owners, hello, 0)
    for other in extra:
        pl.semaphore_signal(barrier, inc=1, device_id=(tile, other), device_id_type=MESH)
    return barrier, owners - 1 + len(extra)


def split3(x):
    high = x.astype(jnp.bfloat16)
    rest = x - high.astype(jnp.float32)
    mid = rest.astype(jnp.bfloat16)
    return high, mid, (rest - mid.astype(jnp.float32)).astype(jnp.bfloat16)


def exchange(src, dst, sems, k, device):
    return pltpu.make_async_remote_copy(
        src_ref=src, dst_ref=dst, send_sem=sems.at[0, k], recv_sem=sems.at[1, k],
        device_id=device, device_id_type=MESH,
    )


def fetch_kernel(dims, want_ref, coef_ref, part_ref, held_ref, asked_ref,
                 asks, answer, landed, first, summed, second, tile_sems, back_sems, attr_sems):
    owners, owned, cap, message, stride = dims
    f32 = jnp.float32
    tile, attr = lax.axis_index("tile"), lax.axis_index("attr")
    core = attr + 1 - 2 * (attr % 2)
    across = (attr + 2) % 4
    pl.semaphore_wait(*greet((tile, attr, owners, (core, across))))

    colour_one = exchange(part_ref, first, attr_sems, 0, (tile, core))
    colour_one.start()

    def ask(other, sender):
        return pltpu.make_async_remote_copy(
            src_ref=want_ref.at[other], dst_ref=asks.at[sender],
            send_sem=tile_sems.at[0, other], recv_sem=tile_sems.at[1, sender],
            device_id=(other, attr), device_id_type=MESH,
        )

    def send_ask(step, _):
        ask((tile + step) % owners, tile).start()
        return 0

    lax.fori_loop(1, owners, send_ask, 0)
    asks[tile] = want_ref[tile]

    colour_one.wait()
    summed[...] = part_ref[...] + first[...]
    colour_two = exchange(summed, second, attr_sems, 1, (tile, across))
    colour_two.start()

    def take_ask(step, _):
        other = (tile + step) % owners
        ask(other, other).wait()
        return 0

    lax.fori_loop(1, owners, take_ask, 0)

    per = 128 // stride
    lanes = owners // per
    rows = []
    for tile_at in range(lanes):
        rows.append(functools.reduce(jnp.add, [asks[tile_at * per + k] for k in range(per)]))
    asked = jnp.concatenate(rows, axis=1) - 1.0
    asked_ref[...] = asked
    wide = 9 * owned
    columns = []
    for tile_at in range(lanes):
        square = jnp.concatenate([rows[tile_at] - 1.0] * 16, axis=0)
        columns.append(jnp.transpose(square)[:, 0:1])
    column = jnp.concatenate(columns, axis=0)
    lane = lax.broadcasted_iota(jnp.int32, (owners * stride, wide), 1).astype(f32)
    pick = jnp.where(lane == column, 1.0, 0.0).astype(jnp.bfloat16)

    colour_two.wait()
    colour = summed[...] + second[...] + 0.5
    table = jnp.concatenate([coef_ref[...], colour], axis=0)
    high, mid, low = split3(table)
    answer[...] = (dot(pick, low) + dot(pick, mid)) + dot(pick, high)

    def back(other, sender):
        at = pl.multiple_of(other * stride, 8)
        return pltpu.make_async_remote_copy(
            src_ref=answer.at[pl.ds(at, message)], dst_ref=landed.at[sender],
            send_sem=back_sems.at[0, other], recv_sem=back_sems.at[1, sender],
            device_id=(other, attr), device_id_type=MESH,
        )

    def send_back(step, _):
        back((tile + step) % owners, tile).start()
        return 0

    lax.fori_loop(1, owners, send_back, 0)
    landed[tile] = answer[pl.ds(pl.multiple_of(tile * stride, 8), message), :]
    held_ref[...] = jnp.zeros_like(held_ref)

    def take_back(step, _):
        other = (tile + step) % owners
        back(other, other).wait()
        return 0

    lax.fori_loop(1, owners, take_back, 0)

    def unpack(o, _):
        for k in range(cap):
            held_ref[o * cap + k, 0:9, :] = landed[o, 9 * k : 9 * k + 9, :]
        return 0

    lax.fori_loop(0, owners, unpack, 0)


def give_kernel(dims, grads_ref, asked_ref, out_ref,
                packed, landed, sums, first, half, second, third, tile_sems, attr_sems):
    owners, owned, cap, message, stride = dims
    f32 = jnp.float32
    tile, attr = lax.axis_index("tile"), lax.axis_index("attr")
    core = attr + 1 - 2 * (attr % 2)
    across = (attr + 2) % 4
    mine = attr % 2

    if message < stride:
        landed[...] = jnp.zeros_like(landed)
    greeted = greet((tile, attr, owners, (core, across)))
    packed[...] = jnp.zeros_like(packed)

    def pack(o, _):
        for k in range(cap):
            packed[o, 9 * k : 9 * k + 6, :] = grads_ref[o * cap + k, 8:14, :]
            packed[o, 9 * k + 6 : 9 * k + 9, :] = grads_ref[o * cap + k, 0:3, :]
        return 0

    lax.fori_loop(0, owners, pack, 0)
    pl.semaphore_wait(*greeted)

    def give(other, sender):
        at = pl.multiple_of(sender * stride, 8)
        return pltpu.make_async_remote_copy(
            src_ref=packed.at[other], dst_ref=landed.at[pl.ds(at, message)],
            send_sem=tile_sems.at[0, other], recv_sem=tile_sems.at[1, sender],
            device_id=(other, attr), device_id_type=MESH,
        )

    def send_give(step, _):
        give((tile + step) % owners, tile).start()
        return 0

    lax.fori_loop(1, owners, send_give, 0)
    landed[pl.ds(pl.multiple_of(tile * stride, 8), message), :] = packed[tile]
    wide = 9 * owned
    row = lax.broadcasted_iota(jnp.int32, (wide, owners * stride), 0).astype(f32)
    pick = jnp.where(row == asked_ref[0:1, :], 1.0, 0.0).astype(jnp.bfloat16)

    def take_give(step, _):
        other = (tile + step) % owners
        give(other, other).wait()
        return 0

    lax.fori_loop(1, owners, take_give, 0)
    high, mid, low = split3(landed[...])
    total = (dot(pick, low) + dot(pick, mid)) + dot(pick, high)
    cut = wide // 2
    sums[0] = total[:cut]
    sums[1] = total[cut:]

    one = exchange(sums.at[1 - mine], first, attr_sems, 0, (tile, core))
    one.start()
    one.wait()
    half[...] = sums[mine] + first[...]
    two = exchange(half, second, attr_sems, 1, (tile, across))
    two.start()
    two.wait()
    half_sum = half[...] + second[...]
    first[...] = half_sum
    three = exchange(first, third, attr_sems, 2, (tile, core))
    three.start()
    three.wait()
    at = pl.multiple_of(mine * cut, 8)
    out_ref[pl.ds(at, cut), :] = half_sum
    at = pl.multiple_of((1 - mine) * cut, 8)
    out_ref[pl.ds(at, cut), :] = third[...]


def remote_call(kernel, dims, outs, ins, scratch, number, name):
    vmem = pl.BlockSpec(memory_space=pltpu.VMEM)
    return pl.pallas_call(
        functools.partial(kernel, dims),
        name=name,
        out_shape=tuple(jax.ShapeDtypeStruct(o, jnp.float32) for o in outs),
        in_specs=[vmem] * len(ins),
        out_specs=tuple(vmem for _ in outs),
        scratch_shapes=scratch,
        compiler_params=pltpu.CompilerParams(
            collective_id=number, has_side_effects=True, vmem_limit_bytes=20 * 1024 * 1024
        ),
    )(*ins)


def floats(*shape):
    return pltpu.VMEM(shape, jnp.float32)


def fetch(dims, want, coef, part):
    owners, owned, cap, message, stride = dims
    sems = pltpu.SemaphoreType.DMA
    return remote_call(
        fetch_kernel, dims,
        ((owners * cap, 16, BLOCK), (8, owners * stride)),
        (want, coef, part),
        [floats(owners, 8, 128), floats(owners * stride, BLOCK), floats(owners, message, BLOCK),
         floats(3 * owned, BLOCK), floats(3 * owned, BLOCK), floats(3 * owned, BLOCK),
         sems((2, owners)), sems((2, owners)), sems((2, 2))],
        1, "fetch",
    )


def give_back(dims, grads, asked):
    owners, owned, cap, message, stride = dims
    sems = pltpu.SemaphoreType.DMA
    cut = 9 * owned // 2
    return remote_call(
        give_kernel, dims, ((9 * owned, BLOCK),), (grads, asked),
        [floats(owners, message, BLOCK), floats(owners * stride, BLOCK), floats(2, cut, BLOCK),
         floats(cut, BLOCK), floats(cut, BLOCK), floats(cut, BLOCK), floats(cut, BLOCK),
         sems((2, owners)), sems((2, 3))],
        2, "give",
    )[0]


def prep_kernel(owned, bands, geometry_ref, angles_ref, coeffs_ref, coef_ref, part_ref, basis_ref, terms_ref,
                geo, ang, coe, rows):
    def relay(b, _):
        for h in range(BLOCK // 128):
            at = pl.ds(pl.multiple_of(b * BLOCK + h * 128, 128), 128)
            geo[h, pl.ds(pl.multiple_of(b * 8, 8), 6), :] = geometry_ref[:, at]
            ang[h, pl.ds(pl.multiple_of(b * 8, 8), 2), :] = angles_ref[:, at]
            coe[h, pl.ds(pl.multiple_of(b * 16, 8), 3 * bands), :] = coeffs_ref[:, at]
        return 0

    lax.fori_loop(0, owned, relay, 0, unroll=4)

    def plane(ref, k, pitch):
        halves = [ref[h, pl.ds(k, owned, stride=pitch), :] for h in range(BLOCK // 128)]
        return jnp.concatenate(halves, axis=1)

    terms = splat_terms([plane(geo, k, 8) for k in range(6)])
    for k, value in enumerate(terms):
        terms_ref[k] = value
    for k, value in enumerate(exponent_rows(terms)):
        coef_ref[k * owned : (k + 1) * owned, :] = value
    for k, value in enumerate(sh_basis([plane(ang, k, 8) for k in range(2)])):
        rows[k] = value
    first = lax.axis_index("attr") * bands
    total = [jnp.zeros((owned, BLOCK), jnp.float32) for _ in range(3)]
    for k in range(bands):
        value = rows[first + k]
        basis_ref[k] = value
        for c in range(3):
            total[c] = total[c] + value * plane(coe, 3 * k + c, 16)
    for c in range(3):
        part_ref[c * owned : (c + 1) * owned, :] = total[c]


def prep(geometry, view_angles, sh_coeffs, owned):
    bands = sh_coeffs.shape[0] // 3
    vmem = pl.BlockSpec(memory_space=pltpu.VMEM)
    shapes = ((6 * owned, BLOCK), (3 * owned, BLOCK), (bands, owned, BLOCK), (11, owned, BLOCK))
    return pl.pallas_call(
        functools.partial(prep_kernel, owned, bands),
        name="prep",
        out_shape=tuple(jax.ShapeDtypeStruct(o, jnp.float32) for o in shapes),
        in_specs=[vmem] * 3,
        out_specs=(vmem,) * 4,
        scratch_shapes=[
            floats(BLOCK // 128, 8 * owned, 128),
            floats(BLOCK // 128, 8 * owned, 128),
            floats(BLOCK // 128, 16 * owned, 128),
            floats(16, owned, BLOCK),
        ],
        compiler_params=pltpu.CompilerParams(vmem_limit_bytes=12 * 1024 * 1024),
    )(geometry, view_angles, sh_coeffs)


def final_kernel(owned, bands, sums_ref, terms_ref, basis_ref, geometry_ref, coeffs_ref, geo, coe):
    summed = [sums_ref[k * owned : (k + 1) * owned, :] for k in range(9)]

    def put(ref, k, pitch, value):
        for h in range(BLOCK // 128):
            ref[h, pl.ds(k, owned, stride=pitch), :] = value[:, h * 128 : (h + 1) * 128]

    for k, value in enumerate(geometry_grads([terms_ref[k] for k in range(11)], summed[:6])):
        put(geo, k, 8, value)
    for k in range(bands):
        for c in range(3):
            put(coe, 3 * k + c, 16, basis_ref[k] * summed[6 + c])

    def relay(b, _):
        for h in range(BLOCK // 128):
            at = pl.ds(pl.multiple_of(b * BLOCK + h * 128, 128), 128)
            geometry_ref[:, at] = geo[h, pl.ds(pl.multiple_of(b * 8, 8), 6), :]
            coeffs_ref[:, at] = coe[h, pl.ds(pl.multiple_of(b * 16, 8), 3 * bands), :]
        return 0

    lax.fori_loop(0, owned, relay, 0, unroll=4)


def final(sums, terms, basis, owned):
    bands = basis.shape[0]
    vmem = pl.BlockSpec(memory_space=pltpu.VMEM)
    shapes = ((6, owned * BLOCK), (3 * bands, owned * BLOCK))
    return pl.pallas_call(
        functools.partial(final_kernel, owned, bands),
        name="final",
        out_shape=tuple(jax.ShapeDtypeStruct(o, jnp.float32) for o in shapes),
        in_specs=[vmem] * 3,
        out_specs=(vmem,) * 2,
        scratch_shapes=[
            floats(BLOCK // 128, 8 * owned, 128),
            floats(BLOCK // 128, 16 * owned, 128),
        ],
        compiler_params=pltpu.CompilerParams(vmem_limit_bytes=12 * 1024 * 1024),
    )(sums, terms, basis)


def local(geometry, sh_coeffs, view_angles, visible, counts, order, image_cot):
    owners = lax.axis_size("tile")
    owned = geometry.shape[1] // BLOCK
    vis = visible.shape[1]
    cap = (vis + owners - 1) // owners
    coef, partial_colour, my_basis, terms = prep(geometry, view_angles, sh_coeffs, owned)

    ids = visible[0]
    owner_of, local_of = ids // owned, ids % owned
    position = jnp.arange(vis)
    rank = jnp.sum(((owner_of[None, :] == owner_of[:, None]) & (position[None, :] < position[:, None])).astype(jnp.int32), 1)
    slot = owner_of * cap + rank
    message = -(-9 * cap // 8) * 8
    stride = 16 if message <= 16 else 32
    dims = (owners, owned, cap, message, stride)
    lane = jnp.arange(128) - (lax.axis_index("tile") % (128 // stride)) * stride
    in_slot = lane[None, :, None] // 9 + jnp.arange(owners)[:, None, None] * cap
    hit = (slot[None, None, :] == in_slot) & (lane >= 0)[None, :, None] & (lane < 9 * cap)[None, :, None]
    want = jnp.sum(jnp.where(hit, 1 + local_of[None, None, :] + owned * (lane % 9)[None, :, None], 0), 2)
    want = jnp.broadcast_to(want.astype(jnp.float32)[:, None, :], (owners, 8, 128))
    slot_of = jnp.sum(jnp.where(visible[:, :, None] == ids[None, None, :], slot[None, None, :], 0), 2)
    seq = jnp.sum(jnp.where(order[:, :, None] == position[None, None, :], slot_of[:, None, :], 0), 2)

    held, asked = fetch(dims, want, coef, partial_colour)
    picture, grads = blend(seq, counts, held, image_cot)
    sums = give_back(dims, grads, asked)
    grad_geometry, grad_sh = final(sums, terms, my_basis, owned)
    return (picture, grad_geometry, grad_sh)


def solution(mesh):
    in_specs = (
        P(None, "tile"),
        P("attr", "tile"),
        P(None, "tile"),
        P(("tile", "attr"), None),
        P(("tile", "attr")),
        P(("tile", "attr"), None),
        P(("tile", "attr"), None, None),
    )
    out_specs = (P(("tile", "attr"), None, None), P(None, "tile"), P("attr", "tile"))
    return jax.shard_map(local, mesh=mesh, in_specs=in_specs, out_specs=out_specs, check_vma=False)
```

profile of v0, /device:TPU:0, one launch (start us, length us, event | category | flops | bytes accessed | tf_op | source)
XLA Modules:
  0.0 63.9 jit_solution(12262667734682696513)
XLA Ops:
  0.6 0.0 copy-start
  0.7 0.7 %fusion.1 = (s32[16]{0:T(128)S(1)}, s32[16]{0:T(128)S(1)}) fusion(s32[2,16]{1,0:T(2,128)} %param.10), kind=kLoop, calls=%fused_computation.20 | loop fusion | flops 192 | bytes 192 | tf_op jit(solution)/shard_map/add | solution.py:587
  1.4 0.7 %and_select_fusion.4 = s32[16]{0:T(128)S(1)} fusion(s32[16]{0:T(128)S(1)} %get-tuple-element.33, s32[2,16]{1,0:T(2,128)} %param.10), kind=kLoop, calls=%fused_computation.13 | loop fusion | flops 192 | bytes 192 | tf_op jit(solution)/shard_map/jit(floor_divide)/jit(_where)/select_n | solution.py:577
  2.1 0.7 %slice_bitcast_fusion = (s32[16]{0:T(128)S(1)}, s32[16]{0:T(128)S(1)}) fusion(s32[2,16]{1,0:T(2,128)} %param.10), kind=kLoop, calls=%fused_computation.29 | loop fusion | flops 240 | bytes 192 | tf_op jit(solution)/shard_map/eq | solution.py:589
  2.8 0.2 convert_reduce_fusion
  3.0 0.9 %select_reduce_fusion.2 = s32[2,16]{1,0:T(2,128)S(1)} fusion(s32[16]{0:T(128)S(1)} %multiply_add_fusion, s32[16]{0:T(128)S(1)} %get-tuple-element.34, s32[2,16]{1,0:T(2,128)} %param.10), kind=kLoop, calls=%fused_computation.2 | loop fusion | flops 1504 | bytes 384 | tf_op jit(solution)/shard_map/reduce_sum | solution.py:589
  3.8 0.9 %select_reduce_fusion.1.seq_ref = s32[2,16]{1,0:T(2,128)S(1)} fusion(s32[2,16]{1,0:T(2,128)S(1)} %select_reduce_fusion.2, s32[2,16]{1,0:T(2,128)} %param.12), kind=kLoop, calls=%fused_computation.1 | loop fusion | flops 1504 | bytes 384 | tf_op jit(solution)/shard_map/reduce_sum | solution.py:590
  4.7 0.1 broadcast_add_fusion.1
  4.8 0.1 broadcast_add_fusion
  4.9 0.1 select_reduce_fusion
  5.0 0.7 %copy.21 = f32[2,256,3]{1,2,0:T(4,128)S(1)} copy(f32[2,256,3]{1,0,2:T(2,128)} %bitcast.12) | data formatting | bytes 12288
  5.7 0.7 %copy.17 = f32[2,3,256]{2,1,0:T(4,128)S(1)} copy(f32[2,3,256]{2,0,1:T(2,128)} %param.13) | data formatting | bytes 12288 | tf_op args[6]
  6.4 0.0 copy-start.1
  6.4 0.0 copy-start.2
  6.5 0.1 copy.19.cot_cols_ref
  6.6 0.0 copy-done
  6.6 0.8 %copy-done.1 = f32[6,8192]{1,0:T(8,128)S(1)} copy-done((f32[6,8192]{1,0:T(8,128)S(1)}, f32[6,8192]{1,0:T(8,128)}, u32[]{:S(2)}) %copy-start.1) | copy-done | bytes 196632
  7.4 0.0 copy-done.2
  7.4 0.8 %prep.1 = (f32[192,256]{1,0:T(8,128)S(1)}, f32[96,256]{1,0:T(8,128)S(1)}, f32[4,32,256]{2,1,0:T(8,128)S(1)}, f32[11,32,256]{2,1,0:T(8,128)S(1)}) custom-call(f32[6,8192]{1,0:T(8,128)S(1)} %copy-done.1, f32[2,8192]{1,0:T(2,128)S(1)} %copy-done.2, f32[12,8192]{1,0:T(8,128)S(1)} %copy-done), custom_call_target="tpu_custom_call" | custom-call | tf_op jit(solution)/shard_map/prep/pallas_call | solution.py:512
  8.2 16.6 %fetch.1 = (f32[16,16,256]{2,1,0:T(8,128)S(1)}, f32[8,256]{1,0:T(8,128)S(1)}) custom-call(f32[8,8,128]{2,1,0:T(8,128)S(1)} %broadcast_in_dim.37.want_ref, f32[192,256]{1,0:T(8,128)S(1)} %get-tuple-element.13.coef_ref, f32[96,256]{1,0:T(8,128)S(1)} %get-tuple-element.14.part_ref), custom_call_target="tpu_custom_call" | custom-call | tf_op jit(solution)/shard_map/fetch/pallas_call | solution.py:430
  24.7 0.0 copy-start.3
  24.8 0.6 %copy-done.3 = s32[2]{0:T(128)S(1)} copy-done((s32[2]{0:T(128)S(1)}, s32[2]{0:T(128)}, u32[]{:S(2)}) %copy-start.3) | copy-done | bytes 32
  25.4 19.5 %blend.1 = (f32[2,16,256]{2,1,0:T(8,128)S(1)}, f32[16,16,256]{2,1,0:T(8,128)S(1)}) custom-call(s32[2,16]{1,0:T(2,128)S(1)} %select_reduce_fusion.1.seq_ref, s32[2]{0:T(128)S(1)} %copy-done.3, f32[16,16,256]{2,1,0:T(8,128)S(1)} %get-tuple-element.15.held_ref, f32[2,8,256]{2,1,0:T(8,128)S(1)} %pad.8.cot_rows_ref, f32[2,256,96]{2,1,0:T(8,128)S(1)} %copy.19.cot_cols_ref), custom_call_target="tpu_custom_call" | custom-call | tf_op jit(solution)/shard_map/blend/pallas_call | solution.py:180
  44.9 0.6 copy.20
  45.5 17.1 %give.1.sums_ref = f32[288,256]{1,0:T(8,128)S(1)} custom-call(f32[16,16,256]{2,1,0:T(8,128)S(1)} %get-tuple-element.17.grads_ref, f32[8,256]{1,0:T(8,128)S(1)} %get-tuple-element.18.asked_ref), custom_call_target="tpu_custom_call" | custom-call | tf_op jit(solution)/shard_map/give/pallas_call | solution.py:430
  62.6 1.3 %final.1 = (f32[6,8192]{1,0:T(8,128)}, f32[12,8192]{1,0:T(8,128)}) custom-call(f32[288,256]{1,0:T(8,128)S(1)} %give.1.sums_ref, f32[11,32,256]{2,1,0:T(8,128)S(1)} %get-tuple-element.19.terms_ref, f32[4,32,256]{2,1,0:T(8,128)S(1)} %get-tuple-element.20.basis_ref), custom_call_target="tpu_custom_call" | custom-call | tf_op jit(solution)/shard_map/final/pallas_call | solution.py:555
  (10 shorter events, 0.1 us)
Async XLA Ops:
  0.6 6.0 %copy-start = (f32[12,8192]{1,0:T(8,128)S(1)}, f32[12,8192]{1,0:T(8,128)}, u32[]{:S(2)}) copy-start(f32[12,8192]{1,0:T(8,128)} %coeffs_ref.1) | copy-start | bytes 1179652
  6.4 1.0 %copy-start.1 = (f32[6,8192]{1,0:T(8,128)S(1)}, f32[6,8192]{1,0:T(8,128)}, u32[]{:S(2)}) copy-start(f32[6,8192]{1,0:T(8,128)} %geometry_ref.1) | copy-start | bytes 589828
  6.4 0.9 %copy-start.2 = (f32[2,8192]{1,0:T(2,128)S(1)}, f32[2,8192]{1,0:T(2,128)}, u32[]{:S(2)}) copy-start(f32[2,8192]{1,0:T(2,128)} %angles_ref.1) | copy-start | bytes 196612
  24.7 0.7 %copy-start.3 = (s32[2]{0:T(128)S(1)}, s32[2]{0:T(128)}, u32[]{:S(2)}) copy-start(s32[2]{0:T(128)} %counts_ref.1) | copy-start | bytes 28
where the time goes:
time: 64.8 us; the launch traced here: 63.9 us
  Pallas kernels  55.2 us (85%)
  other arithmetic  4.3 us (7%)
  local copies, waits for them, and re-layouts  3.62 us (6%)
  between operations  0.78 us (1%)
    pallas_call x2, Pallas kernels, remote_call(): pl.pallas_call(functools.partial(kernel, dims), name=name, out_shape=tupl...  33.6 us
    pallas_call x1, Pallas kernels, blend(): pl.pallas_call(functools.partial(blend_kernel, tiles), name='blend', out_...  19.5 us
    unnamed x11, local copies, waits for them, and re-layouts  3.44 us

commit v1 on v0

--- a/solution.py
+++ b/solution.py
@@ -566,7 +566,7 @@
     )(sums, terms, basis)
 
 
-def local(geometry, sh_coeffs, view_angles, visible, counts, order, image_cot):
+def local_general(geometry, sh_coeffs, view_angles, visible, counts, order, image_cot):
     owners = lax.axis_size("tile")
     owned = geometry.shape[1] // BLOCK
     vis = visible.shape[1]
@@ -596,6 +596,420 @@
     return (picture, grad_geometry, grad_sh)
 
 
+STEPS = 8
+PAIR = 2
+SLOTS = STEPS * PAIR
+OWNED = 32
+MSG = 24
+TRIPLE = 3
+
+
+def stack3(x):
+    high, mid, low = split3(x)
+    return jnp.concatenate([high, mid, low], axis=0)
+
+
+def lane_halves(x):
+    return [x[:, h * 128 : (h + 1) * 128] for h in range(BLOCK // 128)]
+
+
+def put_rows(ref, rows, value):
+    for h, part in enumerate(lane_halves(value)):
+        ref[h, rows, :] = part
+
+
+def get_rows(ref, rows):
+    return jnp.concatenate([ref[h, rows, :] for h in range(BLOCK // 128)], axis=1)
+
+
+def scatter(ref, at, pitch, value):
+    put_rows(ref, pl.ds(at, STEPS, stride=pitch), value)
+
+
+def gather(ref, at, pitch):
+    return get_rows(ref, pl.ds(at, STEPS, stride=pitch))
+
+
+def tile_of(ref, i, at):
+    return jnp.concatenate([ref[i, h, at : at + 8, :] for h in range(BLOCK // 128)], axis=1)
+
+
+def pixel_monomials(shape, dim):
+    pixel = lax.broadcasted_iota(jnp.int32, shape, dim)
+    kind = lax.broadcasted_iota(jnp.int32, shape, 1 - dim) & 7
+    x = (pixel & (SIDE - 1)).astype(jnp.float32) + (0.5 - MID)
+    y = (pixel // SIDE).astype(jnp.float32) + (0.5 - MID)
+    out = jnp.where(kind == 0, 1.0, 0.0)
+    for k, value in ((1, x), (2, y), (3, x * x), (4, x * y), (5, y * y)):
+        out = jnp.where(kind == k, value, out)
+    return out.astype(jnp.bfloat16)
+
+
+def slot_tables(tile, visible, order, counts_ref):
+    f32 = jnp.float32
+    sub = lax.broadcasted_iota(jnp.int32, (SLOTS, SLOTS), 0)
+    lane = lax.broadcasted_iota(jnp.int32, (SLOTS, SLOTS), 1)
+    diagonal = sub == lane
+    lane_f, sub_f = lane.astype(f32), sub.astype(f32)
+
+    def to_column(row):
+        return jnp.sum(jnp.where(diagonal, row, 0.0), axis=1, keepdims=True)
+
+    def to_row(column):
+        return jnp.sum(jnp.where(diagonal, column, 0.0), axis=0, keepdims=True)
+
+    ids = visible[0:1]
+    owner = ids // OWNED
+    near = owner - tile
+    near = jnp.where(near < 0, near + STEPS, near).astype(f32)
+    ids_f = ids.astype(f32)
+    inside = (ids - owner * OWNED).astype(f32)
+    near_column = to_column(near)
+    second = jnp.sum(jnp.where((near_column == near) & (sub < lane), 1.0, 0.0), axis=0, keepdims=True)
+    slot = second * STEPS + near
+    match = sub_f == slot
+    local_id = jnp.sum(jnp.where(match, inside, 0.0), axis=1, keepdims=True)
+    slot_id = jnp.sum(jnp.where(match, ids_f, 0.0), axis=1, keepdims=True)
+    ahead, live = [], []
+    for t in range(2):
+        listed = to_column(visible[t : t + 1].astype(f32))
+        here = sub == order[t : t + 1]
+        sequence = jnp.sum(jnp.where(here, listed, 0.0), axis=0, keepdims=True)
+        rank = jnp.sum(jnp.where(sequence == slot_id, lane_f, 0.0), axis=1, keepdims=True)
+        ahead.append(jnp.where(to_row(rank) < rank, 1.0, 0.0))
+        live.append(jnp.where(rank < counts_ref[t].astype(f32), 1.0, 0.0))
+    return local_id, ahead, live
+
+
+def fused_kernel(bands, counts_ref, geometry_hbm, angles_hbm, coeffs_hbm, visible_hbm, order_hbm, cot_hbm,
+                 pic_ref, basis_ref, terms_ref, out_ref,
+                 geometry, angles, coeffs, visible, order, cot, geo, ang, coe, rows,
+                 coef, part, first, summed, second, colour,
+                 asks_out, asks, answer, held, w_ref, ratio_ref, loss_ref, c_ref, a_ref,
+                 packed, landed, sums, got_core, half, got_across, got_rest,
+                 local_sems, ask_sems, back_sems, give_sems, attr_sems):
+    f32, bf16 = jnp.float32, jnp.bfloat16
+    tile, attr = lax.axis_index("tile"), lax.axis_index("attr")
+    core = attr + 1 - 2 * (attr % 2)
+    across = (attr + 2) % 4
+    mine = attr % 2
+    greeted = greet((tile, attr, STEPS, (core, across)))
+
+    pairs = ((visible_hbm, visible), (order_hbm, order), (geometry_hbm, geometry), (angles_hbm, angles),
+             (coeffs_hbm, coeffs), (cot_hbm, cot))
+    loads = [pltpu.make_async_copy(a, b, local_sems.at[n]) for n, (a, b) in enumerate(pairs)]
+    for load in loads:
+        load.start()
+
+    asks_out[...] = jnp.zeros_like(asks_out)
+    answer[...] = jnp.zeros_like(answer)
+    loss_ref[...] = jnp.zeros_like(loss_ref)
+    loads[0].wait()
+    loads[1].wait()
+    local_id, ahead, live = slot_tables(tile, visible[...], order[...], counts_ref)
+    lane = lax.broadcasted_iota(jnp.int32, (SLOTS, 128), 1)
+    block = (lane & (OWNED - 1)).astype(f32)
+    wanted = jnp.where((block == local_id) & (lane < TRIPLE * OWNED), 1.0, 0.0)
+    for k in range(PAIR):
+        asks_out[pl.ds(k, STEPS, stride=8), :] = wanted[k * STEPS : (k + 1) * STEPS]
+    for load in loads[2:]:
+        load.wait()
+
+    def relay(b, _):
+        for h in range(BLOCK // 128):
+            at = pl.ds(pl.multiple_of(b * BLOCK + h * 128, 128), 128)
+            geo[h, pl.ds(pl.multiple_of(b * 8, 8), 6), :] = geometry[:, at]
+            ang[h, pl.ds(pl.multiple_of(b * 8, 8), 2), :] = angles[:, at]
+            coe[h, pl.ds(pl.multiple_of(b * 16, 8), 3 * bands), :] = coeffs[:, at]
+        return 0
+
+    lax.fori_loop(0, OWNED, relay, 0, unroll=4)
+
+    def plane(ref, k, pitch):
+        halves = [ref[h, pl.ds(k, OWNED, stride=pitch), :] for h in range(BLOCK // 128)]
+        return jnp.concatenate(halves, axis=1)
+
+    for k, value in enumerate(sh_basis([plane(ang, k, 8) for k in range(2)])):
+        rows[k] = value
+    first_band = attr * bands
+    total = [jnp.zeros((OWNED, BLOCK), f32) for _ in range(3)]
+    for k in range(bands):
+        value = rows[first_band + k]
+        basis_ref[k] = value
+        for c in range(3):
+            total[c] = total[c] + value * plane(coe, 3 * k + c, 16)
+    for c in range(3):
+        part[c * OWNED : (c + 1) * OWNED, :] = total[c]
+    pl.semaphore_wait(*greeted)
+
+    def ask(i):
+        return pltpu.make_async_remote_copy(
+            src_ref=asks_out.at[pl.ds(pl.multiple_of(i * 8, 8), 8)], dst_ref=asks.at[pl.ds(pl.multiple_of(i * 8, 8), 8)],
+            send_sem=ask_sems.at[0, i], recv_sem=ask_sems.at[1, i],
+            device_id=((tile + i) % STEPS, attr), device_id_type=MESH,
+        )
+
+    def back(i):
+        return pltpu.make_async_remote_copy(
+            src_ref=answer.at[:, pl.ds(pl.multiple_of(i * MSG, 8), MSG)], dst_ref=held.at[i],
+            send_sem=back_sems.at[0, i], recv_sem=back_sems.at[1, i],
+            device_id=((tile + STEPS - i) % STEPS, attr), device_id_type=MESH,
+        )
+
+    def give(i):
+        return pltpu.make_async_remote_copy(
+            src_ref=packed.at[i], dst_ref=landed.at[:, pl.ds(pl.multiple_of(i * MSG, 8), MSG)],
+            send_sem=give_sems.at[0, i], recv_sem=give_sems.at[1, i],
+            device_id=((tile + i) % STEPS, attr), device_id_type=MESH,
+        )
+
+    def each(act):
+        def step(i, _):
+            act(i)
+            return 0
+
+        lax.fori_loop(1, STEPS, step, 0)
+
+    each(lambda i: ask(i).start())
+    colour_one = exchange(part, first, attr_sems, 0, (tile, core))
+    colour_one.start()
+    asks[0:8, :] = asks_out[0:8, :]
+
+    terms = splat_terms([plane(geo, k, 8) for k in range(6)])
+    for k, value in enumerate(terms):
+        terms_ref[k] = value
+    for k, value in enumerate(exponent_rows(terms)):
+        coef[k] = stack3(value)
+
+    colour_one.wait()
+    summed[...] = part[...] + first[...]
+    colour_two = exchange(summed, second, attr_sems, 1, (tile, across))
+    colour_two.start()
+
+    each(lambda i: ask(i).wait_recv())
+    picks = jnp.concatenate([asks[pl.ds(k, STEPS, stride=8), :] for k in range(PAIR)], axis=0)
+    pick = picks.astype(bf16)[:, : TRIPLE * OWNED]
+    tall = jnp.concatenate([picks] * TRIPLE + [jnp.zeros((128 - TRIPLE * SLOTS, 128), f32)], axis=0)
+    put = jnp.transpose(tall)[:OWNED, : TRIPLE * SLOTS].astype(bf16)
+
+    def pick_row(values, at):
+        found = dot(pick, values)
+        for k in range(PAIR):
+            scatter(answer, at[k], MSG, found[k * STEPS : (k + 1) * STEPS])
+
+    for r in range(6):
+        pick_row(coef[r], (r, 8 + r))
+    colour_two.wait()
+    for c in range(3):
+        piece = slice(c * OWNED, (c + 1) * OWNED)
+        pick_row(stack3(summed[piece] + second[piece] + 0.5), (16 + c, 20 + c))
+    each(lambda i: back(i).start())
+    held[0] = answer[:, 0:MSG, :]
+
+    row = lax.broadcasted_iota(jnp.int32, (2 * BLOCK, BLOCK), 0) & (BLOCK - 1)
+    col = lax.broadcasted_iota(jnp.int32, (2 * BLOCK, BLOCK), 1)
+    before = jnp.where(row < col, -1.0, 0.0).astype(bf16)
+    upto = jnp.where(row <= col, 1.0, 0.0).astype(bf16)
+    mono_cols = pixel_monomials((PIX, 32), 0)
+    mono_rows = pixel_monomials((8, PIX), 1)
+    slot_lane = lax.broadcasted_iota(jnp.int32, (PIX, 128), 1)
+    eight = lax.broadcasted_iota(jnp.int32, (8, BLOCK), 0)
+    own_rows = [(eight >= 4 * k) & (eight < 4 * k + 3) for k in range(PAIR)]
+
+    def halves(x):
+        high = x.astype(bf16).astype(f32)
+        return high, x - high
+
+    def forward(i, _):
+        @pl.when(i > 0)
+        def _():
+            back(i).wait_recv()
+
+        c_high, c_low = halves(tile_of(held, i, 16))
+        seen = None
+        losses = loss_ref[...]
+        for k in range(PAIR):
+            high, mid, low = [p.astype(f32) for p in split3(tile_of(held, i, 8 * k))]
+            coefs = jnp.concatenate([high, mid, low, jnp.zeros_like(low)], axis=0).astype(bf16)
+            alpha = jnp.exp2(dot(mono_cols, coefs))
+            loss = jnp.log(1.0 - alpha) * -LOG2E
+            keep = dot(split2(loss), before)
+            losses = jnp.where(slot_lane == i + k * STEPS, loss[:, BLOCK - 1 :] - keep[:, BLOCK - 1 :], losses)
+            w2 = split2(alpha * jnp.exp2(keep))
+            w_ref[i, k] = w2
+            ratio_ref[i, k] = alpha * jnp.exp2(loss)
+            lhs = jnp.concatenate([jnp.where(own_rows[k], c_high, 0.0), jnp.where(own_rows[k], c_low, 0.0)], axis=0)
+            lhs = lhs.astype(bf16)
+            contract = (((1,), (1,)), ((), ()))
+            shown = lax.dot_general(lhs, w2[:, :BLOCK], contract, preferred_element_type=f32)
+            shown = shown + lax.dot_general(lhs, w2[:, BLOCK:], contract, preferred_element_type=f32)
+            shown = shown[:8] + shown[8:]
+            seen = shown if seen is None else seen + shown
+        loss_ref[...] = losses
+        put_rows(c_ref, pl.ds(pl.multiple_of(i * 8, 8), 8), seen)
+        return 0
+
+    lax.fori_loop(0, STEPS, forward, 0)
+
+    def by_slot(ref, c):
+        return jnp.concatenate([gather(ref, c + 4 * k, 8) for k in range(PAIR)], axis=0)
+
+    losses = jnp.transpose(loss_ref[...])[:SLOTS]
+    local = [by_slot(c_ref, c) for c in range(3)]
+    spread = [jnp.zeros((SLOTS, PIX), f32) for _ in range(4)]
+    for t in range(2):
+        def earlier(values):
+            out = jnp.zeros((SLOTS, PIX), f32)
+            for s in range(SLOTS):
+                out = out + ahead[t][:, s : s + 1] * values[s : s + 1, :]
+            return out
+
+        through = jnp.exp2(-earlier(losses)) * live[t]
+        shade = jnp.zeros((SLOTS, PIX), f32)
+        for c in range(3):
+            g = cot[c, t : t + 1, :]
+            lit = through * local[c]
+            pic_ref[c, t : t + 1, :] = jnp.sum(lit, axis=0, keepdims=True)
+            shade = shade + lit * g
+            spread[c] = spread[c] + through * g
+        behind = earlier(shade) - jnp.sum(shade, axis=0, keepdims=True)
+        spread[3] = spread[3] + live[t] * behind
+    for c in range(4):
+        for k in range(PAIR):
+            scatter(a_ref, c + 4 * k, 8, spread[c][k * STEPS : (k + 1) * STEPS])
+
+    def backward(n, _):
+        i = (n + 1) % STEPS
+        a = get_rows(a_ref, pl.ds(pl.multiple_of(i * 8, 8), 8))
+        a_high, a_low = halves(a)
+        c_high, c_low = halves(tile_of(held, i, 16))
+        columns = jnp.transpose(jnp.concatenate([a_high, a_low, a_high, a], axis=0))
+        v_lhs = columns.astype(bf16)
+        tint = None
+        for k in range(PAIR):
+            ch, cl = jnp.where(own_rows[k], c_high, 0.0), jnp.where(own_rows[k], c_low, 0.0)
+            v_rhs = jnp.concatenate([ch, ch, cl, jnp.zeros_like(cl)], axis=0).astype(bf16)
+            w2 = w_ref[i, k]
+            w_high, w_low = w2[:, :BLOCK], w2[:, BLOCK:]
+            value = (w_high.astype(f32) + w_low.astype(f32)) * dot(v_lhs, v_rhs)
+            beyond = dot(split2(value), upto) + columns[:, 27 + 4 * k : 28 + 4 * k]
+            d2 = split2(value + ratio_ref[i, k] * beyond)
+            moments = dot(mono_rows, d2[:, :BLOCK]) + dot(mono_rows, d2[:, BLOCK:])
+            put_rows(packed.at[i], pl.ds(8 * k, 8), moments)
+            lhs = jnp.concatenate([jnp.where(own_rows[k], a_high, 0.0), jnp.where(own_rows[k], a_low, 0.0)], axis=0)
+            lhs = lhs.astype(bf16)
+            grads = dot(lhs, w_high) + dot(lhs, w_low)
+            grads = grads[:8] + grads[8:]
+            tint = grads if tint is None else tint + grads
+        put_rows(packed.at[i], pl.ds(16, 8), tint)
+
+        @pl.when(i > 0)
+        def _():
+            give(i).start()
+
+        return 0
+
+    lax.fori_loop(0, STEPS, backward, 0)
+    landed[:, 0:MSG, :] = packed[0]
+    each(lambda i: give(i).wait_recv())
+    cut = 9 * OWNED // 2
+    for r in range(9):
+        at = (r, 8 + r) if r < 6 else (10 + r, 14 + r)
+        found = jnp.concatenate([gather(landed, at[k], MSG) for k in range(PAIR)], axis=0)
+        sums[r * OWNED : (r + 1) * OWNED, :] = dot(put, stack3(found))
+
+    at_mine = pl.multiple_of(mine * cut, 8)
+    at_other = pl.multiple_of((1 - mine) * cut, 8)
+    one = exchange(sums.at[pl.ds(at_other, cut)], got_core, attr_sems, 2, (tile, core))
+    one.start()
+    one.wait()
+    half[...] = sums[pl.ds(at_mine, cut), :] + got_core[...]
+    two = exchange(half, got_across, attr_sems, 3, (tile, across))
+    two.start()
+    two.wait()
+    half_sum = half[...] + got_across[...]
+    half[...] = half_sum
+    three = exchange(half, got_rest, attr_sems, 4, (tile, core))
+    three.start()
+    out_ref[pl.ds(at_mine, cut), :] = half_sum
+    three.wait()
+    out_ref[pl.ds(at_other, cut), :] = got_rest[...]
+    each(lambda i: ask(i).wait_send())
+    each(lambda i: back(i).wait_send())
+    each(lambda i: give(i).wait_send())
+
+
+def fused(geometry, view_angles, sh_coeffs, visible, order, cot, counts):
+    bands = sh_coeffs.shape[0] // 3
+    sems = pltpu.SemaphoreType.DMA
+    vmem = pl.BlockSpec(memory_space=pltpu.VMEM)
+    whole = pl.BlockSpec(memory_space=pl.ANY)
+    ins = (geometry, view_angles, sh_coeffs, visible, order, cot)
+    colours, cut = 3 * OWNED, 9 * OWNED // 2
+    shapes = (cot.shape, (bands, OWNED, BLOCK), (11, OWNED, BLOCK), (9 * OWNED, BLOCK))
+    return pl.pallas_call(
+        functools.partial(fused_kernel, bands),
+        name="splat",
+        out_shape=tuple(jax.ShapeDtypeStruct(o, jnp.float32) for o in shapes),
+        in_specs=[pl.BlockSpec(memory_space=pltpu.SMEM)] + [whole] * len(ins),
+        out_specs=tuple(vmem for _ in shapes),
+        scratch_shapes=[pltpu.VMEM(x.shape, x.dtype) for x in ins] + [
+            floats(BLOCK // 128, 8 * OWNED, 128), floats(BLOCK // 128, 8 * OWNED, 128),
+            floats(BLOCK // 128, 16 * OWNED, 128), floats(16, OWNED, BLOCK),
+            pltpu.VMEM((6, TRIPLE * OWNED, BLOCK), jnp.bfloat16), floats(colours, BLOCK), floats(colours, BLOCK),
+            floats(colours, BLOCK), floats(colours, BLOCK), floats(8, 128),
+            floats(8 * STEPS, 128), floats(8 * STEPS, 128), floats(2, STEPS * MSG, 128), floats(STEPS, 2, MSG, 128),
+            pltpu.VMEM((STEPS, PAIR, PIX, 2 * BLOCK), jnp.bfloat16), floats(STEPS, PAIR, PIX, BLOCK),
+            floats(PIX, 128), floats(2, 8 * STEPS, 128), floats(2, 8 * STEPS, 128),
+            floats(STEPS, 2, MSG, 128), floats(2, STEPS * MSG, 128), floats(9 * OWNED, BLOCK),
+            floats(cut, BLOCK), floats(cut, BLOCK), floats(cut, BLOCK), floats(cut, BLOCK),
+            sems((len(ins),)), sems((2, STEPS)), sems((2, STEPS)), sems((2, STEPS)), sems((2, 5)),
+        ],
+        compiler_params=pltpu.CompilerParams(
+            collective_id=3, has_side_effects=True, vmem_limit_bytes=40 * 1024 * 1024
+        ),
+    )(counts, *ins)
+
+
+def finish_kernel(bands, sums_ref, terms_ref, basis_ref, pic_ref, geometry_ref, coeffs_ref, picture_ref, geo, coe):
+    final_kernel(OWNED, bands, sums_ref, terms_ref, basis_ref, geometry_ref, coeffs_ref, geo, coe)
+    picture_ref[...] = pic_ref[...]
+
+
+def finish(sums, terms, basis, pic):
+    bands = basis.shape[0]
+    vmem = pl.BlockSpec(memory_space=pltpu.VMEM)
+    shapes = ((6, OWNED * BLOCK), (3 * bands, OWNED * BLOCK), pic.shape)
+    return pl.pallas_call(
+        functools.partial(finish_kernel, bands),
+        name="finish",
+        out_shape=tuple(jax.ShapeDtypeStruct(o, jnp.float32) for o in shapes),
+        in_specs=[vmem] * 4,
+        out_specs=(vmem,) * 3,
+        scratch_shapes=[
+            floats(BLOCK // 128, 8 * OWNED, 128),
+            floats(BLOCK // 128, 16 * OWNED, 128),
+        ],
+        compiler_params=pltpu.CompilerParams(vmem_limit_bytes=12 * 1024 * 1024),
+    )(sums, terms, basis, pic)
+
+
+def local_fused(geometry, sh_coeffs, view_angles, visible, counts, order, image_cot):
+    cot = jnp.swapaxes(image_cot, 0, 1)
+    pic, basis, terms, sums = fused(geometry, view_angles, sh_coeffs, visible, order, cot, counts)
+    grad_geometry, grad_sh, picture = finish(sums, terms, basis, pic)
+    return (jnp.swapaxes(picture, 0, 1), grad_geometry, grad_sh)
+
+
+def local(geometry, sh_coeffs, view_angles, visible, counts, order, image_cot):
+    owners = lax.axis_size("tile")
+    tiles, vis = visible.shape
+    owned = geometry.shape[1] // BLOCK
+    fits = (owners, vis, tiles, owned, lax.axis_size("attr")) == (8, 16, 2, 32, 4)
+    run = local_fused if fits else local_general
+    return run(geometry, sh_coeffs, view_angles, visible, counts, order, image_cot)
+
+
 def solution(mesh):
     in_specs = (
         P(None, "tile"),

time: 64.8 us -> 49.2 us (0.76)
  Pallas kernels: 55.2 us -> 43.3 us
  other arithmetic: 4.3 us -> 0 us
  local copies, waits for them, and re-layouts: 3.62 us -> 4.88 us
    pallas_call x5 -> x2, Pallas kernels: 55.2 us -> 43.3 us  [the longest x1 42.1 us: fused(): pl.pallas_call(functools.partial(fused_kernel, bands), name='splat', out_...]
    reduce_sum x4 -> x0, other arithmetic: 2 us -> none  [the longest x1 0.86 us: local(): jnp.sum(jnp.where(order[:, :, None] == position[None, None, :], slot_of[:...]
    unnamed x11 -> x14, local copies, waits for them, and re-layouts: 3.44 us -> 4.88 us
    add x4 -> x0, other arithmetic: 0.89 us -> none  [the longest x2 0.81 us: local(): 1 + local_of[None, None, :] + owned * (lane % 9)[None, :, None]]
    select_n x2 -> x0, other arithmetic: 0.71 us -> none  [the longest x1 0.69 us: local(): owner_of, local_of = (ids // owned, ids % owned)]
    eq x1 -> x0, other arithmetic: 0.69 us -> none  [local(): visible[:, :, None] == ids[None, None, :]]
where the time goes in v1:
time: 49.2 us; the launch traced here: 48.9 us
  Pallas kernels  43.3 us (88%)
  local copies, waits for them, and re-layouts  4.88 us (10%)
  between operations  0.66 us (1%)
    pallas_call x1, Pallas kernels, fused(): pl.pallas_call(functools.partial(fused_kernel, bands), name='splat', out_...  42.1 us
    unnamed x14, local copies, waits for them, and re-layouts  4.88 us
    pallas_call x1, Pallas kernels, finish(): pl.pallas_call(functools.partial(finish_kernel, bands), name='finish', ou...  1.26 us

profile of v1, /device:TPU:0, one launch (start us, length us, event | category | flops | bytes accessed | tf_op | source)
XLA Modules:
  0.0 48.9 jit_solution(16711977777755956671)
XLA Ops:
  0.6 0.0 copy-start.6
  0.6 0.0 copy-start.4
  0.7 0.6 %copy-done.6 = s32[2]{0:T(128)S(1)} copy-done((s32[2]{0:T(128)S(1)}, s32[2]{0:T(128)}, u32[]{:S(2)}) %copy-start.6) | copy-done | bytes 32
  1.3 0.0 copy-done.4
  1.3 0.0 copy-start
  1.3 1.0 %copy-done = f32[12,8192]{1,0:T(8,128)S(1)} copy-done((f32[12,8192]{1,0:T(8,128)S(1)}, f32[12,8192]{1,0:T(8,128)}, u32[]{:S(2)}) %copy-start) | copy-done | bytes 393240
  2.4 0.0 copy-start.1
  2.4 0.9 %copy-done.1 = f32[6,8192]{1,0:T(8,128)S(1)} copy-done((f32[6,8192]{1,0:T(8,128)S(1)}, f32[6,8192]{1,0:T(8,128)}, u32[]{:S(2)}) %copy-start.1) | copy-done | bytes 196632
  3.3 0.0 copy-start.2
  3.3 0.8 %copy-done.2 = f32[2,8192]{1,0:T(2,128)S(1)} copy-done((f32[2,8192]{1,0:T(2,128)S(1)}, f32[2,8192]{1,0:T(2,128)}, u32[]{:S(2)}) %copy-start.2) | copy-done | bytes 65560
  4.2 0.0 copy-start.3
  4.2 0.7 %copy-done.3 = f32[2,3,256]{2,0,1:T(2,128)S(1)} copy-done((f32[2,3,256]{2,0,1:T(2,128)S(1)}, f32[2,3,256]{2,0,1:T(2,128)}, u32[]{:S(2)}) %copy-start.3) | copy-done | bytes 6168
  4.9 0.0 copy-start.5
  4.9 0.7 %copy-done.5 = s32[2,16]{1,0:T(2,128)S(1)} copy-done((s32[2,16]{1,0:T(2,128)S(1)}, s32[2,16]{1,0:T(2,128)}, u32[]{:S(2)}) %copy-start.5) | copy-done | bytes 152
  5.5 42.1 %splat.1 = (f32[3,2,256]{2,1,0:T(2,128)S(1)}, f32[4,32,256]{2,1,0:T(8,128)S(1)}, f32[11,32,256]{2,1,0:T(8,128)S(1)}, f32[288,256]{1,0:T(8,128)S(1)}) custom-call(s32[2]{0:T(128)S(1)} %copy-done.6, f32[6,8192]{1,0:T(8,128)S(1)} %copy-done.1, f32[2,8192]{1,0:T(2,128)S(1)} %copy-done.2, f32[12,8192]{1,0:T(8,128)S(1)} %copy-done, s32[2,16]{1,0:T(2,128)S(1)} %copy-done.4, ...), custom_call_target="tpu_custom_call" | custom-call | tf_op jit(solution)/shard_map/splat/pallas_call | solution.py:950
  47.6 1.3 %finish.1 = (f32[6,8192]{1,0:T(8,128)}, f32[12,8192]{1,0:T(8,128)}, f32[3,2,256]{2,1,0:T(2,128)}) custom-call(f32[288,256]{1,0:T(8,128)S(1)} %get-tuple-element.10.sums_ref, f32[11,32,256]{2,1,0:T(8,128)S(1)} %get-tuple-element.11.terms_ref, f32[4,32,256]{2,1,0:T(8,128)S(1)} %get-tuple-element.12.basis_ref, f32[3,2,256]{2,1,0:T(2,128)S(1)} %get-tuple-element.13.pic_ref), custom_call_target="tpu_custom_call" | custom-call | tf_op jit(solution)/shard_map/finish/pallas_call | solution.py:983
Async XLA Ops:
  0.6 0.7 %copy-start.6 = (s32[2]{0:T(128)S(1)}, s32[2]{0:T(128)}, u32[]{:S(2)}) copy-start(s32[2]{0:T(128)} %counts_ref.1) | copy-start | bytes 28
  0.6 0.7 %copy-start.4 = (s32[2,16]{1,0:T(2,128)S(1)}, s32[2,16]{1,0:T(2,128)}, u32[]{:S(2)}) copy-start(s32[2,16]{1,0:T(2,128)} %visible_hbm.1) | copy-start | bytes 388
  1.3 1.0 %copy-start = (f32[12,8192]{1,0:T(8,128)S(1)}, f32[12,8192]{1,0:T(8,128)}, u32[]{:S(2)}) copy-start(f32[12,8192]{1,0:T(8,128)} %coeffs_hbm.1) | copy-start | bytes 1179652
  2.4 0.9 %copy-start.1 = (f32[6,8192]{1,0:T(8,128)S(1)}, f32[6,8192]{1,0:T(8,128)}, u32[]{:S(2)}) copy-start(f32[6,8192]{1,0:T(8,128)} %geometry_hbm.1) | copy-start | bytes 589828
  3.3 0.8 %copy-start.2 = (f32[2,8192]{1,0:T(2,128)S(1)}, f32[2,8192]{1,0:T(2,128)}, u32[]{:S(2)}) copy-start(f32[2,8192]{1,0:T(2,128)} %angles_hbm.1) | copy-start | bytes 196612
  4.2 0.7 %copy-start.3 = (f32[2,3,256]{2,0,1:T(2,128)S(1)}, f32[2,3,256]{2,0,1:T(2,128)}, u32[]{:S(2)}) copy-start(f32[2,3,256]{2,0,1:T(2,128)} %param.13) | copy-start | bytes 18436
  4.9 0.7 %copy-start.5 = (s32[2,16]{1,0:T(2,128)S(1)}, s32[2,16]{1,0:T(2,128)}, u32[]{:S(2)}) copy-start(s32[2,16]{1,0:T(2,128)} %order_hbm.1) | copy-start | bytes 388

commit v2 on v1

--- a/solution.py
+++ b/solution.py
@@ -681,9 +681,9 @@
     return local_id, ahead, live
 
 
-def fused_kernel(bands, counts_ref, geometry_hbm, angles_hbm, coeffs_hbm, visible_hbm, order_hbm, cot_hbm,
+def fused_kernel(bands, geometry_hbm, angles_hbm, coeffs_hbm, visible_hbm, order_hbm, cot_hbm, counts_hbm,
                  pic_ref, basis_ref, terms_ref, out_ref,
-                 geometry, angles, coeffs, visible, order, cot, geo, ang, coe, rows,
+                 geometry, angles, coeffs, visible, order, cot, counts_ref, geo, ang, coe, rows,
                  coef, part, first, summed, second, colour,
                  asks_out, asks, answer, held, w_ref, ratio_ref, loss_ref, c_ref, a_ref,
                  packed, landed, sums, got_core, half, got_across, got_rest,
@@ -695,8 +695,8 @@
     mine = attr % 2
     greeted = greet((tile, attr, STEPS, (core, across)))
 
-    pairs = ((visible_hbm, visible), (order_hbm, order), (geometry_hbm, geometry), (angles_hbm, angles),
-             (coeffs_hbm, coeffs), (cot_hbm, cot))
+    pairs = ((visible_hbm, visible), (order_hbm, order), (counts_hbm, counts_ref), (angles_hbm, angles),
+             (coeffs_hbm, coeffs), (geometry_hbm, geometry), (cot_hbm, cot))
     loads = [pltpu.make_async_copy(a, b, local_sems.at[n]) for n, (a, b) in enumerate(pairs)]
     for load in loads:
         load.start()
@@ -704,15 +704,15 @@
     asks_out[...] = jnp.zeros_like(asks_out)
     answer[...] = jnp.zeros_like(answer)
     loss_ref[...] = jnp.zeros_like(loss_ref)
-    loads[0].wait()
-    loads[1].wait()
+    for load in loads[:3]:
+        load.wait()
     local_id, ahead, live = slot_tables(tile, visible[...], order[...], counts_ref)
     lane = lax.broadcasted_iota(jnp.int32, (SLOTS, 128), 1)
     block = (lane & (OWNED - 1)).astype(f32)
     wanted = jnp.where((block == local_id) & (lane < TRIPLE * OWNED), 1.0, 0.0)
     for k in range(PAIR):
         asks_out[pl.ds(k, STEPS, stride=8), :] = wanted[k * STEPS : (k + 1) * STEPS]
-    for load in loads[2:]:
+    for load in loads[3:]:
         load.wait()
 
     def relay(b, _):
@@ -943,17 +943,17 @@
     bands = sh_coeffs.shape[0] // 3
     sems = pltpu.SemaphoreType.DMA
     vmem = pl.BlockSpec(memory_space=pltpu.VMEM)
-    whole = pl.BlockSpec(memory_space=pl.ANY)
-    ins = (geometry, view_angles, sh_coeffs, visible, order, cot)
+    ins = (geometry, view_angles, sh_coeffs, visible, order, cot, counts)
     colours, cut = 3 * OWNED, 9 * OWNED // 2
     shapes = (cot.shape, (bands, OWNED, BLOCK), (11, OWNED, BLOCK), (9 * OWNED, BLOCK))
     return pl.pallas_call(
         functools.partial(fused_kernel, bands),
         name="splat",
         out_shape=tuple(jax.ShapeDtypeStruct(o, jnp.float32) for o in shapes),
-        in_specs=[pl.BlockSpec(memory_space=pltpu.SMEM)] + [whole] * len(ins),
+        in_specs=[pl.BlockSpec(memory_space=pltpu.HBM)] * len(ins),
         out_specs=tuple(vmem for _ in shapes),
-        scratch_shapes=[pltpu.VMEM(x.shape, x.dtype) for x in ins] + [
+        scratch_shapes=[pltpu.VMEM(x.shape, x.dtype) for x in ins[:-1]] + [
+            pltpu.SMEM(counts.shape, counts.dtype),
             floats(BLOCK // 128, 8 * OWNED, 128), floats(BLOCK // 128, 8 * OWNED, 128),
             floats(BLOCK // 128, 16 * OWNED, 128), floats(16, OWNED, BLOCK),
             pltpu.VMEM((6, TRIPLE * OWNED, BLOCK), jnp.bfloat16), floats(colours, BLOCK), floats(colours, BLOCK),
@@ -968,7 +968,7 @@
         compiler_params=pltpu.CompilerParams(
             collective_id=3, has_side_effects=True, vmem_limit_bytes=40 * 1024 * 1024
         ),
-    )(counts, *ins)
+    )(*[pltpu.with_memory_space_constraint(x, pltpu.HBM) for x in ins])
 
 
 def finish_kernel(bands, sums_ref, terms_ref, basis_ref, pic_ref, geometry_ref, coeffs_ref, picture_ref, geo, coe):

time: 49.2 us -> 43.6 us (0.89)
  local copies, waits for them, and re-layouts: 4.88 us -> 0 us
  Pallas kernels: 43.3 us -> 42.8 us
    unnamed x14 -> x0, local copies, waits for them, and re-layouts: 4.88 us -> none
    pallas_call x1, Pallas kernels: 42.1 us -> 41.5 us  [fused(): pl.pallas_call(functools.partial(fused_kernel, bands), name='splat', out_...]
where the time goes in v2:
time: 43.6 us; the launch traced here: 43.4 us
  Pallas kernels  42.8 us (98%)
  between operations  0.64 us (1%)
    pallas_call x1, Pallas kernels, fused(): pl.pallas_call(functools.partial(fused_kernel, bands), name='splat', out_...  41.5 us
    pallas_call x1, Pallas kernels, finish(): pl.pallas_call(functools.partial(finish_kernel, bands), name='finish', ou...  1.27 us

profile of v2, /device:TPU:0, one launch (start us, length us, event | category | flops | bytes accessed | tf_op | source)
XLA Modules:
  0.0 43.4 jit_solution(2262752169214067830)
XLA Ops:
  0.6 41.5 %splat.1 = (f32[3,2,256]{2,1,0:T(2,128)S(1)}, f32[4,32,256]{2,1,0:T(8,128)S(1)}, f32[11,32,256]{2,1,0:T(8,128)S(1)}, f32[288,256]{1,0:T(8,128)S(1)}) custom-call(f32[6,8192]{1,0:T(8,128)} %geometry_hbm.1, f32[2,8192]{1,0:T(2,128)} %angles_hbm.1, f32[12,8192]{1,0:T(8,128)} %coeffs_hbm.1, s32[2,16]{1,0:T(2,128)} %visible_hbm.1, s32[2,16]{1,0:T(2,128)} %order_hbm.1, ...), custom_call_target="tpu_custom_call" | custom-call | tf_op jit(solution)/shard_map/splat/pallas_call | solution.py:949
  42.2 1.3 %finish.1 = (f32[6,8192]{1,0:T(8,128)}, f32[12,8192]{1,0:T(8,128)}, f32[3,2,256]{2,1,0:T(2,128)}) custom-call(f32[288,256]{1,0:T(8,128)S(1)} %get-tuple-element.10.sums_ref, f32[11,32,256]{2,1,0:T(8,128)S(1)} %get-tuple-element.11.terms_ref, f32[4,32,256]{2,1,0:T(8,128)S(1)} %get-tuple-element.12.basis_ref, f32[3,2,256]{2,1,0:T(2,128)S(1)} %get-tuple-element.13.pic_ref), custom_call_target="tpu_custom_call" | custom-call | tf_op jit(solution)/shard_map/finish/pallas_call | solution.py:983

commit v3 on v2

--- a/solution.py
+++ b/solution.py
@@ -686,14 +686,14 @@
                  geometry, angles, coeffs, visible, order, cot, counts_ref, geo, ang, coe, rows,
                  coef, part, first, summed, second, colour,
                  asks_out, asks, answer, held, w_ref, ratio_ref, loss_ref, c_ref, a_ref,
-                 packed, landed, sums, got_core, half, got_across, got_rest,
-                 local_sems, ask_sems, back_sems, give_sems, attr_sems):
+                 packed, landed, sums, got_core, all_picks, d_ref,
+                 local_sems, ask_sems, back_sems, give_sems, share_sems, attr_sems):
     f32, bf16 = jnp.float32, jnp.bfloat16
     tile, attr = lax.axis_index("tile"), lax.axis_index("attr")
     core = attr + 1 - 2 * (attr % 2)
     across = (attr + 2) % 4
     mine = attr % 2
-    greeted = greet((tile, attr, STEPS, (core, across)))
+    greeted = greet((tile, attr, STEPS, (core, across, (core + 2) % 4)))
 
     pairs = ((visible_hbm, visible), (order_hbm, order), (counts_hbm, counts_ref), (angles_hbm, angles),
              (coeffs_hbm, coeffs), (geometry_hbm, geometry), (cot_hbm, cot))
@@ -756,12 +756,16 @@
             device_id=((tile + STEPS - i) % STEPS, attr), device_id_type=MESH,
         )
 
-    def give(i):
+    def give(i, d):
+        slot = d * STEPS + i
         return pltpu.make_async_remote_copy(
-            src_ref=packed.at[i], dst_ref=landed.at[:, pl.ds(pl.multiple_of(i * MSG, 8), MSG)],
-            send_sem=give_sems.at[0, i], recv_sem=give_sems.at[1, i],
-            device_id=((tile + i) % STEPS, attr), device_id_type=MESH,
+            src_ref=packed.at[i, (attr + d) % 2], dst_ref=landed.at[pl.ds(pl.multiple_of(slot * MSG, 8), MSG)],
+            send_sem=give_sems.at[0, slot], recv_sem=give_sems.at[1, slot],
+            device_id=((tile + i) % STEPS, (attr + d) % 4), device_id_type=MESH,
         )
+
+    def share(d):
+        return exchange(all_picks.at[0], all_picks.at[d], share_sems, d, (tile, (attr + d) % 4))
 
     def each(act):
         def step(i, _):
@@ -789,8 +793,9 @@
     each(lambda i: ask(i).wait_recv())
     picks = jnp.concatenate([asks[pl.ds(k, STEPS, stride=8), :] for k in range(PAIR)], axis=0)
     pick = picks.astype(bf16)[:, : TRIPLE * OWNED]
-    tall = jnp.concatenate([picks] * TRIPLE + [jnp.zeros((128 - TRIPLE * SLOTS, 128), f32)], axis=0)
-    put = jnp.transpose(tall)[:OWNED, : TRIPLE * SLOTS].astype(bf16)
+    all_picks[0] = picks
+    for d in range(1, 4):
+        share(d).start()
 
     def pick_row(values, at):
         found = dot(pick, values)
@@ -820,13 +825,7 @@
         high = x.astype(bf16).astype(f32)
         return high, x - high
 
-    def forward(i, _):
-        @pl.when(i > 0)
-        def _():
-            back(i).wait_recv()
-
-        c_high, c_low = halves(tile_of(held, i, 16))
-        seen = None
+    def shape_pair(i):
         losses = loss_ref[...]
         for k in range(PAIR):
             high, mid, low = [p.astype(f32) for p in split3(tile_of(held, i, 8 * k))]
@@ -835,9 +834,15 @@
             loss = jnp.log(1.0 - alpha) * -LOG2E
             keep = dot(split2(loss), before)
             losses = jnp.where(slot_lane == i + k * STEPS, loss[:, BLOCK - 1 :] - keep[:, BLOCK - 1 :], losses)
-            w2 = split2(alpha * jnp.exp2(keep))
-            w_ref[i, k] = w2
+            w_ref[i, k] = split2(alpha * jnp.exp2(keep))
             ratio_ref[i, k] = alpha * jnp.exp2(loss)
+        loss_ref[...] = losses
+
+    def show_pair(i):
+        c_high, c_low = halves(tile_of(held, i, 16))
+        seen = None
+        for k in range(PAIR):
+            w2 = w_ref[i, k]
             lhs = jnp.concatenate([jnp.where(own_rows[k], c_high, 0.0), jnp.where(own_rows[k], c_low, 0.0)], axis=0)
             lhs = lhs.astype(bf16)
             contract = (((1,), (1,)), ((), ()))
@@ -845,11 +850,17 @@
             shown = shown + lax.dot_general(lhs, w2[:, BLOCK:], contract, preferred_element_type=f32)
             shown = shown[:8] + shown[8:]
             seen = shown if seen is None else seen + shown
-        loss_ref[...] = losses
         put_rows(c_ref, pl.ds(pl.multiple_of(i * 8, 8), 8), seen)
-        return 0
-
-    lax.fori_loop(0, STEPS, forward, 0)
+
+    def forward(i, _):
+        back(i).wait_recv()
+        show_pair(i - 1)
+        shape_pair(i)
+        return 0
+
+    shape_pair(0)
+    lax.fori_loop(1, STEPS, forward, 0)
+    show_pair(STEPS - 1)
 
     def by_slot(ref, c):
         return jnp.concatenate([gather(ref, c + 4 * k, 8) for k in range(PAIR)], axis=0)
@@ -878,65 +889,88 @@
         for k in range(PAIR):
             scatter(a_ref, c + 4 * k, 8, spread[c][k * STEPS : (k + 1) * STEPS])
 
-    def backward(n, _):
-        i = (n + 1) % STEPS
+    def slope_pair(i):
         a = get_rows(a_ref, pl.ds(pl.multiple_of(i * 8, 8), 8))
         a_high, a_low = halves(a)
         c_high, c_low = halves(tile_of(held, i, 16))
         columns = jnp.transpose(jnp.concatenate([a_high, a_low, a_high, a], axis=0))
         v_lhs = columns.astype(bf16)
-        tint = None
         for k in range(PAIR):
             ch, cl = jnp.where(own_rows[k], c_high, 0.0), jnp.where(own_rows[k], c_low, 0.0)
             v_rhs = jnp.concatenate([ch, ch, cl, jnp.zeros_like(cl)], axis=0).astype(bf16)
             w2 = w_ref[i, k]
-            w_high, w_low = w2[:, :BLOCK], w2[:, BLOCK:]
-            value = (w_high.astype(f32) + w_low.astype(f32)) * dot(v_lhs, v_rhs)
+            value = (w2[:, :BLOCK].astype(f32) + w2[:, BLOCK:].astype(f32)) * dot(v_lhs, v_rhs)
             beyond = dot(split2(value), upto) + columns[:, 27 + 4 * k : 28 + 4 * k]
-            d2 = split2(value + ratio_ref[i, k] * beyond)
+            d_ref[k] = split2(value + ratio_ref[i, k] * beyond)
+
+    def sum_pair(i):
+        a_high, a_low = halves(get_rows(a_ref, pl.ds(pl.multiple_of(i * 8, 8), 8)))
+        tint = None
+        for k in range(PAIR):
+            d2, w2 = d_ref[k], w_ref[i, k]
             moments = dot(mono_rows, d2[:, :BLOCK]) + dot(mono_rows, d2[:, BLOCK:])
             put_rows(packed.at[i], pl.ds(8 * k, 8), moments)
             lhs = jnp.concatenate([jnp.where(own_rows[k], a_high, 0.0), jnp.where(own_rows[k], a_low, 0.0)], axis=0)
             lhs = lhs.astype(bf16)
-            grads = dot(lhs, w_high) + dot(lhs, w_low)
+            grads = dot(lhs, w2[:, :BLOCK]) + dot(lhs, w2[:, BLOCK:])
             grads = grads[:8] + grads[8:]
             tint = grads if tint is None else tint + grads
         put_rows(packed.at[i], pl.ds(16, 8), tint)
 
-        @pl.when(i > 0)
-        def _():
-            give(i).start()
-
-        return 0
-
-    lax.fori_loop(0, STEPS, backward, 0)
-    landed[:, 0:MSG, :] = packed[0]
-    each(lambda i: give(i).wait_recv())
-    cut = 9 * OWNED // 2
-    for r in range(9):
-        at = (r, 8 + r) if r < 6 else (10 + r, 14 + r)
-        found = jnp.concatenate([gather(landed, at[k], MSG) for k in range(PAIR)], axis=0)
-        sums[r * OWNED : (r + 1) * OWNED, :] = dot(put, stack3(found))
-
-    at_mine = pl.multiple_of(mine * cut, 8)
-    at_other = pl.multiple_of((1 - mine) * cut, 8)
-    one = exchange(sums.at[pl.ds(at_other, cut)], got_core, attr_sems, 2, (tile, core))
-    one.start()
-    one.wait()
-    half[...] = sums[pl.ds(at_mine, cut), :] + got_core[...]
-    two = exchange(half, got_across, attr_sems, 3, (tile, across))
-    two.start()
-    two.wait()
-    half_sum = half[...] + got_across[...]
-    half[...] = half_sum
-    three = exchange(half, got_rest, attr_sems, 4, (tile, core))
-    three.start()
-    out_ref[pl.ds(at_mine, cut), :] = half_sum
-    three.wait()
-    out_ref[pl.ds(at_other, cut), :] = got_rest[...]
+    def backward(n, _):
+        sum_pair(n)
+        slope_pair((n + 1) % STEPS)
+        for d in range(4):
+            give(n, d).start()
+        return 0
+
+    slope_pair(1)
+    lax.fori_loop(1, STEPS, backward, 0)
+    sum_pair(0)
+    for d in range(1, 4):
+        give(0, d).start()
+    landed[0:MSG, :] = packed[0, mine]
+
+    for d in range(1, 4):
+        share(d).wait_recv()
+    chosen = [all_picks[d, k * STEPS : (k + 1) * STEPS, :] for k in range(PAIR) for d in range(4)]
+    tall = jnp.concatenate(chosen * TRIPLE + [jnp.zeros((256 - TRIPLE * 4 * SLOTS, 128), f32)], axis=0)
+    put = jnp.transpose(tall)[:OWNED, : TRIPLE * 4 * SLOTS].astype(bf16)
+
+    def take_give(n, _):
+        for d in range(4):
+            give(n, d).wait_recv()
+        return 0
+
+    lax.fori_loop(1, STEPS, take_give, 0)
+    for d in range(1, 4):
+        give(0, d).wait_recv()
+    for r in range(0, 9, 2):
+        both = []
+        for q in range(r, min(r + 2, 9)):
+            at = (q, 8 + q) if q < 6 else (10 + q, 14 + q)
+            both.append(jnp.concatenate([landed[pl.ds(at[k], 4 * STEPS, stride=MSG), :] for k in range(PAIR)], axis=0))
+        found = dot(put, stack3(jnp.concatenate(both, axis=1)))
+        for q in range(len(both)):
+            sums[(r + q) * OWNED : (r + q + 1) * OWNED, :] = found[:, q * 128 : (q + 1) * 128]
+
+    swap = exchange(sums, got_core, attr_sems, 2, (tile, core))
+    swap.start()
+    out_ref[mine] = sums[...]
+    for d in range(1, 4):
+        share(d).wait_send()
+        give(0, d).wait_send()
+
+    def sent_give(n, _):
+        for d in range(4):
+            give(n, d).wait_send()
+        return 0
+
+    lax.fori_loop(1, STEPS, sent_give, 0)
     each(lambda i: ask(i).wait_send())
     each(lambda i: back(i).wait_send())
-    each(lambda i: give(i).wait_send())
+    swap.wait()
+    out_ref[1 - mine] = got_core[...]
 
 
 def fused(geometry, view_angles, sh_coeffs, visible, order, cot, counts):
@@ -944,8 +978,8 @@
     sems = pltpu.SemaphoreType.DMA
     vmem = pl.BlockSpec(memory_space=pltpu.VMEM)
     ins = (geometry, view_angles, sh_coeffs, visible, order, cot, counts)
-    colours, cut = 3 * OWNED, 9 * OWNED // 2
-    shapes = (cot.shape, (bands, OWNED, BLOCK), (11, OWNED, BLOCK), (9 * OWNED, BLOCK))
+    colours = 3 * OWNED
+    shapes = (cot.shape, (bands, OWNED, BLOCK), (11, OWNED, BLOCK), (2, 9 * OWNED, 128))
     return pl.pallas_call(
         functools.partial(fused_kernel, bands),
         name="splat",
@@ -961,9 +995,9 @@
             floats(8 * STEPS, 128), floats(8 * STEPS, 128), floats(2, STEPS * MSG, 128), floats(STEPS, 2, MSG, 128),
             pltpu.VMEM((STEPS, PAIR, PIX, 2 * BLOCK), jnp.bfloat16), floats(STEPS, PAIR, PIX, BLOCK),
             floats(PIX, 128), floats(2, 8 * STEPS, 128), floats(2, 8 * STEPS, 128),
-            floats(STEPS, 2, MSG, 128), floats(2, STEPS * MSG, 128), floats(9 * OWNED, BLOCK),
-            floats(cut, BLOCK), floats(cut, BLOCK), floats(cut, BLOCK), floats(cut, BLOCK),
-            sems((len(ins),)), sems((2, STEPS)), sems((2, STEPS)), sems((2, STEPS)), sems((2, 5)),
+            floats(STEPS, 2, MSG, 128), floats(4 * STEPS * MSG, 128), floats(9 * OWNED, 128), floats(9 * OWNED, 128),
+            floats(4, SLOTS, 128), pltpu.VMEM((PAIR, PIX, 2 * BLOCK), jnp.bfloat16),
+            sems((len(ins),)), sems((2, STEPS)), sems((2, STEPS)), sems((2, 4 * STEPS)), sems((2, 4)), sems((2, 3)),
         ],
         compiler_params=pltpu.CompilerParams(
             collective_id=3, has_side_effects=True, vmem_limit_bytes=40 * 1024 * 1024
@@ -971,8 +1005,10 @@
     )(*[pltpu.with_memory_space_constraint(x, pltpu.HBM) for x in ins])
 
 
-def finish_kernel(bands, sums_ref, terms_ref, basis_ref, pic_ref, geometry_ref, coeffs_ref, picture_ref, geo, coe):
-    final_kernel(OWNED, bands, sums_ref, terms_ref, basis_ref, geometry_ref, coeffs_ref, geo, coe)
+def finish_kernel(bands, sums_ref, terms_ref, basis_ref, pic_ref, geometry_ref, coeffs_ref, picture_ref, both, geo, coe):
+    for h in range(BLOCK // 128):
+        both[:, h * 128 : (h + 1) * 128] = sums_ref[h]
+    final_kernel(OWNED, bands, both, terms_ref, basis_ref, geometry_ref, coeffs_ref, geo, coe)
     picture_ref[...] = pic_ref[...]
 
 
@@ -987,6 +1023,7 @@
         in_specs=[vmem] * 4,
         out_specs=(vmem,) * 3,
         scratch_shapes=[
+            floats(9 * OWNED, BLOCK),
             floats(BLOCK // 128, 8 * OWNED, 128),
             floats(BLOCK // 128, 16 * OWNED, 128),
         ],

time: 43.6 us -> 34.7 us (0.80)
  Pallas kernels: 42.8 us -> 33.6 us
    pallas_call x1, Pallas kernels: 41.5 us -> 32.3 us  [fused(): pl.pallas_call(functools.partial(fused_kernel, bands), name='splat', out_...]
where the time goes in v3:
time: 34.7 us; the launch traced here: 34.2 us
  Pallas kernels  33.6 us (97%)
  between operations  0.64 us (2%)
    pallas_call x1, Pallas kernels, fused(): pl.pallas_call(functools.partial(fused_kernel, bands), name='splat', out_...  32.3 us
    pallas_call x1, Pallas kernels, finish(): pl.pallas_call(functools.partial(finish_kernel, bands), name='finish', ou...  1.26 us

profile of v3, /device:TPU:0, one launch (start us, length us, event | category | flops | bytes accessed | tf_op | source)
XLA Modules:
  0.0 34.2 jit_solution(7934784419983008499)
XLA Ops:
  0.6 32.3 %splat.1 = (f32[3,2,256]{2,1,0:T(2,128)S(1)}, f32[4,32,256]{2,1,0:T(8,128)S(1)}, f32[11,32,256]{2,1,0:T(8,128)S(1)}, f32[2,288,128]{2,1,0:T(8,128)S(1)}) custom-call(f32[6,8192]{1,0:T(8,128)} %geometry_hbm.1, f32[2,8192]{1,0:T(2,128)} %angles_hbm.1, f32[12,8192]{1,0:T(8,128)} %coeffs_hbm.1, s32[2,16]{1,0:T(2,128)} %visible_hbm.1, s32[2,16]{1,0:T(2,128)} %order_hbm.1, ...), custom_call_target="tpu_custom_call" | custom-call | tf_op jit(solution)/shard_map/splat/pallas_call | solution.py:983
  33.0 1.3 %finish.1 = (f32[6,8192]{1,0:T(8,128)}, f32[12,8192]{1,0:T(8,128)}, f32[3,2,256]{2,1,0:T(2,128)}) custom-call(f32[2,288,128]{2,1,0:T(8,128)S(1)} %get-tuple-element.10.sums_ref, f32[11,32,256]{2,1,0:T(8,128)S(1)} %get-tuple-element.11.terms_ref, f32[4,32,256]{2,1,0:T(8,128)S(1)} %get-tuple-element.12.basis_ref, f32[3,2,256]{2,1,0:T(2,128)S(1)} %get-tuple-element.13.pic_ref), custom_call_target="tpu_custom_call" | custom-call | tf_op jit(solution)/shard_map/finish/pallas_call | solution.py:1019

commit v4 on v3

--- a/solution.py
+++ b/solution.py
@@ -602,6 +602,7 @@
 OWNED = 32
 MSG = 24
 TRIPLE = 3
+LAG = 3
 
 
 def stack3(x):
@@ -685,7 +686,7 @@
                  pic_ref, basis_ref, terms_ref, out_ref,
                  geometry, angles, coeffs, visible, order, cot, counts_ref, geo, ang, coe, rows,
                  coef, part, first, summed, second, colour,
-                 asks_out, asks, answer, held, w_ref, ratio_ref, loss_ref, c_ref, a_ref,
+                 asks_out, asks, answer, held, w_ref, ratio_ref, c_ref, a_ref,
                  packed, landed, sums, got_core, all_picks, d_ref,
                  local_sems, ask_sems, back_sems, give_sems, share_sems, attr_sems):
     f32, bf16 = jnp.float32, jnp.bfloat16
@@ -703,7 +704,6 @@
 
     asks_out[...] = jnp.zeros_like(asks_out)
     answer[...] = jnp.zeros_like(answer)
-    loss_ref[...] = jnp.zeros_like(loss_ref)
     for load in loads[:3]:
         load.wait()
     local_id, ahead, live = slot_tables(tile, visible[...], order[...], counts_ref)
@@ -749,10 +749,11 @@
             device_id=((tile + i) % STEPS, attr), device_id_type=MESH,
         )
 
-    def back(i):
+    def back(i, part):
+        at, size = ((0, 16), (16, 8))[part]
         return pltpu.make_async_remote_copy(
-            src_ref=answer.at[:, pl.ds(pl.multiple_of(i * MSG, 8), MSG)], dst_ref=held.at[i],
-            send_sem=back_sems.at[0, i], recv_sem=back_sems.at[1, i],
+            src_ref=answer.at[:, pl.ds(pl.multiple_of(i * MSG + at, 8), size)], dst_ref=held.at[i, :, pl.ds(at, size)],
+            send_sem=back_sems.at[0, part, i], recv_sem=back_sems.at[1, part, i],
             device_id=((tile + STEPS - i) % STEPS, attr), device_id_type=MESH,
         )
 
@@ -767,9 +768,17 @@
     def share(d):
         return exchange(all_picks.at[0], all_picks.at[d], share_sems, d, (tile, (attr + d) % 4))
 
+    upper = tile // (STEPS // 2)
+
+    def near(n):
+        return (n + upper * (STEPS - 2 * n)) % STEPS
+
+    def far(n):
+        return (STEPS - n + upper * (2 * n - STEPS)) % STEPS
+
     def each(act):
-        def step(i, _):
-            act(i)
+        def step(n, _):
+            act(far(n))
             return 0
 
         lax.fori_loop(1, STEPS, step, 0)
@@ -804,12 +813,8 @@
 
     for r in range(6):
         pick_row(coef[r], (r, 8 + r))
-    colour_two.wait()
-    for c in range(3):
-        piece = slice(c * OWNED, (c + 1) * OWNED)
-        pick_row(stack3(summed[piece] + second[piece] + 0.5), (16 + c, 20 + c))
-    each(lambda i: back(i).start())
-    held[0] = answer[:, 0:MSG, :]
+    each(lambda i: back(i, 0).start())
+    held[0, :, 0:16] = answer[:, 0:16, :]
 
     row = lax.broadcasted_iota(jnp.int32, (2 * BLOCK, BLOCK), 0) & (BLOCK - 1)
     col = lax.broadcasted_iota(jnp.int32, (2 * BLOCK, BLOCK), 1)
@@ -817,7 +822,6 @@
     upto = jnp.where(row <= col, 1.0, 0.0).astype(bf16)
     mono_cols = pixel_monomials((PIX, 32), 0)
     mono_rows = pixel_monomials((8, PIX), 1)
-    slot_lane = lax.broadcasted_iota(jnp.int32, (PIX, 128), 1)
     eight = lax.broadcasted_iota(jnp.int32, (8, BLOCK), 0)
     own_rows = [(eight >= 4 * k) & (eight < 4 * k + 3) for k in range(PAIR)]
 
@@ -826,24 +830,26 @@
         return high, x - high
 
     def shape_pair(i):
-        losses = loss_ref[...]
+        alphas, losses = [], []
         for k in range(PAIR):
             high, mid, low = [p.astype(f32) for p in split3(tile_of(held, i, 8 * k))]
             coefs = jnp.concatenate([high, mid, low, jnp.zeros_like(low)], axis=0).astype(bf16)
             alpha = jnp.exp2(dot(mono_cols, coefs))
             loss = jnp.log(1.0 - alpha) * -LOG2E
-            keep = dot(split2(loss), before)
-            losses = jnp.where(slot_lane == i + k * STEPS, loss[:, BLOCK - 1 :] - keep[:, BLOCK - 1 :], losses)
-            w_ref[i, k] = split2(alpha * jnp.exp2(keep))
+            alphas.append(alpha)
+            losses.append(split2(loss))
             ratio_ref[i, k] = alpha * jnp.exp2(loss)
-        loss_ref[...] = losses
+        keep = dot(jnp.concatenate(losses, axis=0), before)
+        for k in range(PAIR):
+            w_ref[i, k] = split2(alphas[k] * jnp.exp2(keep[k * PIX : (k + 1) * PIX]))
 
     def show_pair(i):
         c_high, c_low = halves(tile_of(held, i, 16))
         seen = None
         for k in range(PAIR):
             w2 = w_ref[i, k]
-            lhs = jnp.concatenate([jnp.where(own_rows[k], c_high, 0.0), jnp.where(own_rows[k], c_low, 0.0)], axis=0)
+            one = jnp.where(eight == 4 * k + 3, 1.0, 0.0)
+            lhs = jnp.concatenate([jnp.where(own_rows[k], c_high, one), jnp.where(own_rows[k], c_low, 0.0)], axis=0)
             lhs = lhs.astype(bf16)
             contract = (((1,), (1,)), ((), ()))
             shown = lax.dot_general(lhs, w2[:, :BLOCK], contract, preferred_element_type=f32)
@@ -852,21 +858,42 @@
             seen = shown if seen is None else seen + shown
         put_rows(c_ref, pl.ds(pl.multiple_of(i * 8, 8), 8), seen)
 
-    def forward(i, _):
-        back(i).wait_recv()
-        show_pair(i - 1)
+    def forward_early(n, _):
+        i = near(n)
+        back(i, 0).wait_recv()
         shape_pair(i)
         return 0
 
+    def forward(n, _):
+        i, shown = near(n), near(n - LAG)
+        back(i, 0).wait_recv()
+
+        @pl.when(n > LAG)
+        def _():
+            back(shown, 1).wait_recv()
+
+        show_pair(shown)
+        shape_pair(i)
+        return 0
+
     shape_pair(0)
-    lax.fori_loop(1, STEPS, forward, 0)
-    show_pair(STEPS - 1)
+    colour_two.wait()
+    for c in range(3):
+        piece = slice(c * OWNED, (c + 1) * OWNED)
+        pick_row(stack3(summed[piece] + second[piece] + 0.5), (16 + c, 20 + c))
+    each(lambda i: back(i, 1).start())
+    held[0, :, 16:24] = answer[:, 16:24, :]
+    lax.fori_loop(1, LAG, forward_early, 0)
+    lax.fori_loop(LAG, STEPS, forward, 0)
+    for n in range(STEPS - LAG, STEPS):
+        back(near(n), 1).wait_recv()
+    for n in range(STEPS - LAG, STEPS):
+        show_pair(near(n))
 
     def by_slot(ref, c):
         return jnp.concatenate([gather(ref, c + 4 * k, 8) for k in range(PAIR)], axis=0)
 
-    losses = jnp.transpose(loss_ref[...])[:SLOTS]
-    local = [by_slot(c_ref, c) for c in range(3)]
+    local = [by_slot(c_ref, c) for c in range(4)]
     spread = [jnp.zeros((SLOTS, PIX), f32) for _ in range(4)]
     for t in range(2):
         def earlier(values):
@@ -875,7 +902,9 @@
                 out = out + ahead[t][:, s : s + 1] * values[s : s + 1, :]
             return out
 
-        through = jnp.exp2(-earlier(losses)) * live[t]
+        through = jnp.broadcast_to(live[t], (SLOTS, PIX))
+        for s in range(SLOTS):
+            through = through * (1.0 - ahead[t][:, s : s + 1] * local[3][s : s + 1, :])
         shade = jnp.zeros((SLOTS, PIX), f32)
         for c in range(3):
             g = cot[c, t : t + 1, :]
@@ -895,13 +924,16 @@
         c_high, c_low = halves(tile_of(held, i, 16))
         columns = jnp.transpose(jnp.concatenate([a_high, a_low, a_high, a], axis=0))
         v_lhs = columns.astype(bf16)
+        values = []
         for k in range(PAIR):
             ch, cl = jnp.where(own_rows[k], c_high, 0.0), jnp.where(own_rows[k], c_low, 0.0)
             v_rhs = jnp.concatenate([ch, ch, cl, jnp.zeros_like(cl)], axis=0).astype(bf16)
             w2 = w_ref[i, k]
-            value = (w2[:, :BLOCK].astype(f32) + w2[:, BLOCK:].astype(f32)) * dot(v_lhs, v_rhs)
-            beyond = dot(split2(value), upto) + columns[:, 27 + 4 * k : 28 + 4 * k]
-            d_ref[k] = split2(value + ratio_ref[i, k] * beyond)
+            values.append((w2[:, :BLOCK].astype(f32) + w2[:, BLOCK:].astype(f32)) * dot(v_lhs, v_rhs))
+        total = dot(jnp.concatenate([split2(value) for value in values], axis=0), upto)
+        for k in range(PAIR):
+            beyond = total[k * PIX : (k + 1) * PIX] + columns[:, 27 + 4 * k : 28 + 4 * k]
+            d_ref[k] = split2(values[k] + ratio_ref[i, k] * beyond)
 
     def sum_pair(i):
         a_high, a_low = halves(get_rows(a_ref, pl.ds(pl.multiple_of(i * 8, 8), 8)))
@@ -918,13 +950,14 @@
         put_rows(packed.at[i], pl.ds(16, 8), tint)
 
     def backward(n, _):
-        sum_pair(n)
-        slope_pair((n + 1) % STEPS)
+        i = far(n)
+        sum_pair(i)
+        slope_pair(far(n + 1))
         for d in range(4):
-            give(n, d).start()
-        return 0
-
-    slope_pair(1)
+            give(i, d).start()
+        return 0
+
+    slope_pair(far(1))
     lax.fori_loop(1, STEPS, backward, 0)
     sum_pair(0)
     for d in range(1, 4):
@@ -968,7 +1001,8 @@
 
     lax.fori_loop(1, STEPS, sent_give, 0)
     each(lambda i: ask(i).wait_send())
-    each(lambda i: back(i).wait_send())
+    each(lambda i: back(i, 0).wait_send())
+    each(lambda i: back(i, 1).wait_send())
     swap.wait()
     out_ref[1 - mine] = got_core[...]
 
@@ -994,10 +1028,10 @@
             floats(colours, BLOCK), floats(colours, BLOCK), floats(8, 128),
             floats(8 * STEPS, 128), floats(8 * STEPS, 128), floats(2, STEPS * MSG, 128), floats(STEPS, 2, MSG, 128),
             pltpu.VMEM((STEPS, PAIR, PIX, 2 * BLOCK), jnp.bfloat16), floats(STEPS, PAIR, PIX, BLOCK),
-            floats(PIX, 128), floats(2, 8 * STEPS, 128), floats(2, 8 * STEPS, 128),
+            floats(2, 8 * STEPS, 128), floats(2, 8 * STEPS, 128),
             floats(STEPS, 2, MSG, 128), floats(4 * STEPS * MSG, 128), floats(9 * OWNED, 128), floats(9 * OWNED, 128),
             floats(4, SLOTS, 128), pltpu.VMEM((PAIR, PIX, 2 * BLOCK), jnp.bfloat16),
-            sems((len(ins),)), sems((2, STEPS)), sems((2, STEPS)), sems((2, 4 * STEPS)), sems((2, 4)), sems((2, 3)),
+            sems((len(ins),)), sems((2, STEPS)), sems((2, 2, STEPS)), sems((2, 4 * STEPS)), sems((2, 4)), sems((2, 3)),
         ],
         compiler_params=pltpu.CompilerParams(
             collective_id=3, has_side_effects=True, vmem_limit_bytes=40 * 1024 * 1024

time: 34.7 us -> 32.6 us (0.939)
  the two profiles are of different devices: /device:TPU:0 before, /device:TPU:13 now
where the time goes in v4:
time: 32.6 us; the launch traced here: 32.4 us
  Pallas kernels  31.8 us (98%)
  between operations  0.64 us (2%)
    pallas_call x1, Pallas kernels, fused(): pl.pallas_call(functools.partial(fused_kernel, bands), name='splat', out_...  30.5 us
    pallas_call x1, Pallas kernels, finish(): pl.pallas_call(functools.partial(finish_kernel, bands), name='finish', ou...  1.26 us

profile of v4, /device:TPU:13, one launch (start us, length us, event | category | flops | bytes accessed | tf_op | source)
XLA Modules:
  0.0 32.4 jit_solution(5258409016517292963)
XLA Ops:
  0.6 30.5 %splat.1 = (f32[3,2,256]{2,1,0:T(2,128)S(1)}, f32[4,32,256]{2,1,0:T(8,128)S(1)}, f32[11,32,256]{2,1,0:T(8,128)S(1)}, f32[2,288,128]{2,1,0:T(8,128)S(1)}) custom-call(f32[6,8192]{1,0:T(8,128)} %geometry_hbm.1, f32[2,8192]{1,0:T(2,128)} %angles_hbm.1, f32[12,8192]{1,0:T(8,128)} %coeffs_hbm.1, s32[2,16]{1,0:T(2,128)} %visible_hbm.1, s32[2,16]{1,0:T(2,128)} %order_hbm.1, ...), custom_call_target="tpu_custom_call" | custom-call | tf_op jit(solution)/shard_map/splat/pallas_call | solution.py:1017
  31.1 1.3 %finish.1 = (f32[6,8192]{1,0:T(8,128)}, f32[12,8192]{1,0:T(8,128)}, f32[3,2,256]{2,1,0:T(2,128)}) custom-call(f32[2,288,128]{2,1,0:T(8,128)S(1)} %get-tuple-element.10.sums_ref, f32[11,32,256]{2,1,0:T(8,128)S(1)} %get-tuple-element.11.terms_ref, f32[4,32,256]{2,1,0:T(8,128)S(1)} %get-tuple-element.12.basis_ref, f32[3,2,256]{2,1,0:T(2,128)S(1)} %get-tuple-element.13.pic_ref), custom_call_target="tpu_custom_call" | custom-call | tf_op jit(solution)/shard_map/finish/pallas_call | solution.py:1053

commit v5 on v4

--- a/solution.py
+++ b/solution.py
@@ -603,6 +603,7 @@
 MSG = 24
 TRIPLE = 3
 LAG = 3
+GIVEN = 9 * PAIR
 
 
 def stack3(x):
@@ -760,7 +761,8 @@
     def give(i, d):
         slot = d * STEPS + i
         return pltpu.make_async_remote_copy(
-            src_ref=packed.at[i, (attr + d) % 2], dst_ref=landed.at[pl.ds(pl.multiple_of(slot * MSG, 8), MSG)],
+            src_ref=packed.at[i, (attr + d) % 2, pl.ds(0, GIVEN)],
+            dst_ref=landed.at[pl.ds(pl.multiple_of(slot * MSG, 8), GIVEN)],
             send_sem=give_sems.at[0, slot], recv_sem=give_sems.at[1, slot],
             device_id=((tile + i) % STEPS, (attr + d) % 4), device_id_type=MESH,
         )
@@ -937,17 +939,17 @@
 
     def sum_pair(i):
         a_high, a_low = halves(get_rows(a_ref, pl.ds(pl.multiple_of(i * 8, 8), 8)))
-        tint = None
+        moments, tint = [], None
         for k in range(PAIR):
             d2, w2 = d_ref[k], w_ref[i, k]
-            moments = dot(mono_rows, d2[:, :BLOCK]) + dot(mono_rows, d2[:, BLOCK:])
-            put_rows(packed.at[i], pl.ds(8 * k, 8), moments)
+            moments.append(dot(mono_rows, d2[:, :BLOCK]) + dot(mono_rows, d2[:, BLOCK:]))
             lhs = jnp.concatenate([jnp.where(own_rows[k], a_high, 0.0), jnp.where(own_rows[k], a_low, 0.0)], axis=0)
             lhs = lhs.astype(bf16)
             grads = dot(lhs, w2[:, :BLOCK]) + dot(lhs, w2[:, BLOCK:])
             grads = grads[:8] + grads[8:]
             tint = grads if tint is None else tint + grads
-        put_rows(packed.at[i], pl.ds(16, 8), tint)
+        pieces = [m[:6] for m in moments] + [tint[0:3], tint[4:7], jnp.zeros((6, BLOCK), f32)]
+        put_rows(packed.at[i], pl.ds(0, MSG), jnp.concatenate(pieces, axis=0))
 
     def backward(n, _):
         i = far(n)
@@ -981,7 +983,7 @@
     for r in range(0, 9, 2):
         both = []
         for q in range(r, min(r + 2, 9)):
-            at = (q, 8 + q) if q < 6 else (10 + q, 14 + q)
+            at = (q, 6 + q) if q < 6 else (6 + q, 9 + q)
             both.append(jnp.concatenate([landed[pl.ds(at[k], 4 * STEPS, stride=MSG), :] for k in range(PAIR)], axis=0))
         found = dot(put, stack3(jnp.concatenate(both, axis=1)))
         for q in range(len(both)):

time: 32.6 us -> 30.7 us (0.942)
  the two profiles are of different devices: /device:TPU:13 before, /device:TPU:0 now
where the time goes in v5:
time: 30.7 us; the launch traced here: 30.5 us
  Pallas kernels  29.9 us (97%)
  between operations  0.64 us (2%)
    pallas_call x1, Pallas kernels, fused(): pl.pallas_call(functools.partial(fused_kernel, bands), name='splat', out_...  28.6 us
    pallas_call x1, Pallas kernels, finish(): pl.pallas_call(functools.partial(finish_kernel, bands), name='finish', ou...  1.26 us

profile of v5, /device:TPU:0, one launch (start us, length us, event | category | flops | bytes accessed | tf_op | source)
XLA Modules:
  0.0 30.5 jit_solution(462738498844713613)
XLA Ops:
  0.6 28.6 %splat.1 = (f32[3,2,256]{2,1,0:T(2,128)S(1)}, f32[4,32,256]{2,1,0:T(8,128)S(1)}, f32[11,32,256]{2,1,0:T(8,128)S(1)}, f32[2,288,128]{2,1,0:T(8,128)S(1)}) custom-call(f32[6,8192]{1,0:T(8,128)} %geometry_hbm.1, f32[2,8192]{1,0:T(2,128)} %angles_hbm.1, f32[12,8192]{1,0:T(8,128)} %coeffs_hbm.1, s32[2,16]{1,0:T(2,128)} %visible_hbm.1, s32[2,16]{1,0:T(2,128)} %order_hbm.1, ...), custom_call_target="tpu_custom_call" | custom-call | tf_op jit(solution)/shard_map/splat/pallas_call | solution.py:1019
  29.2 1.3 %finish.1 = (f32[6,8192]{1,0:T(8,128)}, f32[12,8192]{1,0:T(8,128)}, f32[3,2,256]{2,1,0:T(2,128)}) custom-call(f32[2,288,128]{2,1,0:T(8,128)S(1)} %get-tuple-element.10.sums_ref, f32[11,32,256]{2,1,0:T(8,128)S(1)} %get-tuple-element.11.terms_ref, f32[4,32,256]{2,1,0:T(8,128)S(1)} %get-tuple-element.12.basis_ref, f32[3,2,256]{2,1,0:T(2,128)S(1)} %get-tuple-element.13.pic_ref), custom_call_target="tpu_custom_call" | custom-call | tf_op jit(solution)/shard_map/finish/pallas_call | solution.py:1055

commit v6 on v5

--- a/solution.py
+++ b/solution.py
@@ -688,7 +688,7 @@
                  geometry, angles, coeffs, visible, order, cot, counts_ref, geo, ang, coe, rows,
                  coef, part, first, summed, second, colour,
                  asks_out, asks, answer, held, w_ref, ratio_ref, c_ref, a_ref,
-                 packed, landed, sums, got_core, all_picks, d_ref,
+                 packed, landed, sums, got_core, all_picks, d_ref, columns_ref,
                  local_sems, ask_sems, back_sems, give_sems, share_sems, attr_sems):
     f32, bf16 = jnp.float32, jnp.bfloat16
     tile, attr = lax.axis_index("tile"), lax.axis_index("attr")
@@ -776,7 +776,7 @@
         return (n + upper * (STEPS - 2 * n)) % STEPS
 
     def far(n):
-        return (STEPS - n + upper * (2 * n - STEPS)) % STEPS
+        return (2 * STEPS - n + upper * (2 * n - STEPS)) % STEPS
 
     def each(act):
         def step(n, _):
@@ -785,9 +785,9 @@
 
         lax.fori_loop(1, STEPS, step, 0)
 
-    each(lambda i: ask(i).start())
     colour_one = exchange(part, first, attr_sems, 0, (tile, core))
     colour_one.start()
+    each(lambda i: ask(i).start())
     asks[0:8, :] = asks_out[0:8, :]
 
     terms = splat_terms([plane(geo, k, 8) for k in range(6)])
@@ -831,12 +831,18 @@
         high = x.astype(bf16).astype(f32)
         return high, x - high
 
-    def shape_pair(i):
-        alphas, losses = [], []
+    def powers_of(i):
+        powers = []
         for k in range(PAIR):
             high, mid, low = [p.astype(f32) for p in split3(tile_of(held, i, 8 * k))]
             coefs = jnp.concatenate([high, mid, low, jnp.zeros_like(low)], axis=0).astype(bf16)
-            alpha = jnp.exp2(dot(mono_cols, coefs))
+            powers.append(dot(mono_cols, coefs))
+        return powers
+
+    def shape_pair(i, powers):
+        alphas, losses = [], []
+        for k in range(PAIR):
+            alpha = jnp.exp2(powers[k])
             loss = jnp.log(1.0 - alpha) * -LOG2E
             alphas.append(alpha)
             losses.append(split2(loss))
@@ -863,7 +869,7 @@
     def forward_early(n, _):
         i = near(n)
         back(i, 0).wait_recv()
-        shape_pair(i)
+        shape_pair(i, powers_of(i))
         return 0
 
     def forward(n, _):
@@ -874,11 +880,12 @@
         def _():
             back(shown, 1).wait_recv()
 
+        powers = powers_of(i)
         show_pair(shown)
-        shape_pair(i)
-        return 0
-
-    shape_pair(0)
+        shape_pair(i, powers)
+        return 0
+
+    shape_pair(0, powers_of(0))
     colour_two.wait()
     for c in range(3):
         piece = slice(c * OWNED, (c + 1) * OWNED)
@@ -920,18 +927,24 @@
         for k in range(PAIR):
             scatter(a_ref, c + 4 * k, 8, spread[c][k * STEPS : (k + 1) * STEPS])
 
-    def slope_pair(i):
+    def turn(i):
         a = get_rows(a_ref, pl.ds(pl.multiple_of(i * 8, 8), 8))
         a_high, a_low = halves(a)
+        columns_ref[...] = jnp.transpose(jnp.concatenate([a_high, a_low, a_high, a], axis=0))
+
+    def tints_of(i, columns):
         c_high, c_low = halves(tile_of(held, i, 16))
-        columns = jnp.transpose(jnp.concatenate([a_high, a_low, a_high, a], axis=0))
-        v_lhs = columns.astype(bf16)
+        tints = []
+        for k in range(PAIR):
+            ch, cl = jnp.where(own_rows[k], c_high, 0.0), jnp.where(own_rows[k], c_low, 0.0)
+            tints.append(dot(columns.astype(bf16), jnp.concatenate([ch, ch, cl, jnp.zeros_like(cl)], axis=0).astype(bf16)))
+        return tints
+
+    def slope_pair(i, columns, tints):
         values = []
         for k in range(PAIR):
-            ch, cl = jnp.where(own_rows[k], c_high, 0.0), jnp.where(own_rows[k], c_low, 0.0)
-            v_rhs = jnp.concatenate([ch, ch, cl, jnp.zeros_like(cl)], axis=0).astype(bf16)
             w2 = w_ref[i, k]
-            values.append((w2[:, :BLOCK].astype(f32) + w2[:, BLOCK:].astype(f32)) * dot(v_lhs, v_rhs))
+            values.append((w2[:, :BLOCK].astype(f32) + w2[:, BLOCK:].astype(f32)) * tints[k])
         total = dot(jnp.concatenate([split2(value) for value in values], axis=0), upto)
         for k in range(PAIR):
             beyond = total[k * PIX : (k + 1) * PIX] + columns[:, 27 + 4 * k : 28 + 4 * k]
@@ -952,14 +965,20 @@
         put_rows(packed.at[i], pl.ds(0, MSG), jnp.concatenate(pieces, axis=0))
 
     def backward(n, _):
-        i = far(n)
+        i, after = far(n), far(n + 1)
+        columns = columns_ref[...]
+        tints = tints_of(after, columns)
         sum_pair(i)
-        slope_pair(far(n + 1))
+        slope_pair(after, columns, tints)
+        turn(far(n + 2))
         for d in range(4):
             give(i, d).start()
         return 0
 
-    slope_pair(far(1))
+    turn(far(1))
+    columns = columns_ref[...]
+    slope_pair(far(1), columns, tints_of(far(1), columns))
+    turn(far(2))
     lax.fori_loop(1, STEPS, backward, 0)
     sum_pair(0)
     for d in range(1, 4):
@@ -1032,7 +1051,7 @@
             pltpu.VMEM((STEPS, PAIR, PIX, 2 * BLOCK), jnp.bfloat16), floats(STEPS, PAIR, PIX, BLOCK),
             floats(2, 8 * STEPS, 128), floats(2, 8 * STEPS, 128),
             floats(STEPS, 2, MSG, 128), floats(4 * STEPS * MSG, 128), floats(9 * OWNED, 128), floats(9 * OWNED, 128),
-            floats(4, SLOTS, 128), pltpu.VMEM((PAIR, PIX, 2 * BLOCK), jnp.bfloat16),
+            floats(4, SLOTS, 128), pltpu.VMEM((PAIR, PIX, 2 * BLOCK), jnp.bfloat16), floats(PIX, 32),
             sems((len(ins),)), sems((2, STEPS)), sems((2, 2, STEPS)), sems((2, 4 * STEPS)), sems((2, 4)), sems((2, 3)),
         ],
         compiler_params=pltpu.CompilerParams(
@@ -1041,11 +1060,41 @@
     )(*[pltpu.with_memory_space_constraint(x, pltpu.HBM) for x in ins])
 
 
-def finish_kernel(bands, sums_ref, terms_ref, basis_ref, pic_ref, geometry_ref, coeffs_ref, picture_ref, both, geo, coe):
-    for h in range(BLOCK // 128):
-        both[:, h * 128 : (h + 1) * 128] = sums_ref[h]
-    final_kernel(OWNED, bands, both, terms_ref, basis_ref, geometry_ref, coeffs_ref, geo, coe)
-    picture_ref[...] = pic_ref[...]
+def finish_kernel(bands, sums_ref, terms_ref, basis_ref, pic_ref, geometry_hbm, coeffs_hbm, picture_hbm,
+                  geo, coe, geometry_ref, coeffs_ref, sems):
+    pairs = ((pic_ref, picture_hbm), (coeffs_ref, coeffs_hbm), (geometry_ref, geometry_hbm))
+    stores = [pltpu.make_async_copy(a, b, sems.at[n]) for n, (a, b) in enumerate(pairs)]
+    stores[0].start()
+
+    def summed(r):
+        return jnp.concatenate([sums_ref[h, r * OWNED : (r + 1) * OWNED, :] for h in range(BLOCK // 128)], axis=1)
+
+    def put(ref, k, pitch, value):
+        for h, part in enumerate(lane_halves(value)):
+            ref[h, pl.ds(k, OWNED, stride=pitch), :] = part
+
+    def relay(ref, out, pitch, count):
+        def step(b, _):
+            for h in range(BLOCK // 128):
+                at = pl.ds(pl.multiple_of(b * BLOCK + h * 128, 128), 128)
+                out[:, at] = ref[h, pl.ds(pl.multiple_of(b * pitch, 8), count), :]
+            return 0
+
+        lax.fori_loop(0, OWNED, step, 0, unroll=4)
+
+    for c in range(3):
+        tint = summed(6 + c)
+        for k in range(bands):
+            put(coe, 3 * k + c, 16, basis_ref[k] * tint)
+    relay(coe, coeffs_ref, 16, 3 * bands)
+    stores[1].start()
+    grads = geometry_grads([terms_ref[k] for k in range(11)], [summed(r) for r in range(6)])
+    for k, value in enumerate(grads):
+        put(geo, k, 8, value)
+    relay(geo, geometry_ref, 8, 6)
+    stores[2].start()
+    for store in stores:
+        store.wait()
 
 
 def finish(sums, terms, basis, pic):
@@ -1057,11 +1106,11 @@
         name="finish",
         out_shape=tuple(jax.ShapeDtypeStruct(o, jnp.float32) for o in shapes),
         in_specs=[vmem] * 4,
-        out_specs=(vmem,) * 3,
+        out_specs=tuple(pl.BlockSpec(memory_space=pltpu.HBM) for _ in shapes),
         scratch_shapes=[
-            floats(9 * OWNED, BLOCK),
             floats(BLOCK // 128, 8 * OWNED, 128),
             floats(BLOCK // 128, 16 * OWNED, 128),
+            floats(*shapes[0]), floats(*shapes[1]), pltpu.SemaphoreType.DMA((3,)),
         ],
         compiler_params=pltpu.CompilerParams(vmem_limit_bytes=12 * 1024 * 1024),
     )(sums, terms, basis, pic)

time: 30.7 us -> 30.5 us (level)
  no operation moved by 1% of the time
where the time goes in v6:
time: 30.5 us; the launch traced here: 30.4 us
  Pallas kernels  29.7 us (97%)
  between operations  0.64 us (2%)
    pallas_call x1, Pallas kernels, fused(): pl.pallas_call(functools.partial(fused_kernel, bands), name='splat', out_...  28.5 us
    pallas_call x1, Pallas kernels, finish(): pl.pallas_call(functools.partial(finish_kernel, bands), name='finish', ou...  1.21 us

profile of v6, /device:TPU:0, one launch (start us, length us, event | category | flops | bytes accessed | tf_op | source)
XLA Modules:
  0.0 30.4 jit_solution(4084150432232140335)
XLA Ops:
  0.6 28.5 %splat.1 = (f32[3,2,256]{2,1,0:T(2,128)S(1)}, f32[4,32,256]{2,1,0:T(8,128)S(1)}, f32[11,32,256]{2,1,0:T(8,128)S(1)}, f32[2,288,128]{2,1,0:T(8,128)S(1)}) custom-call(f32[6,8192]{1,0:T(8,128)} %geometry_hbm.1, f32[2,8192]{1,0:T(2,128)} %angles_hbm.1, f32[12,8192]{1,0:T(8,128)} %coeffs_hbm.1, s32[2,16]{1,0:T(2,128)} %visible_hbm.1, s32[2,16]{1,0:T(2,128)} %order_hbm.1, ...), custom_call_target="tpu_custom_call" | custom-call | tf_op jit(solution)/shard_map/splat/pallas_call | solution.py:1038
  29.1 1.2 %finish.1 = (f32[6,8192]{1,0:T(8,128)}, f32[12,8192]{1,0:T(8,128)}, f32[3,2,256]{2,1,0:T(2,128)}) custom-call(f32[2,288,128]{2,1,0:T(8,128)S(1)} %get-tuple-element.10.sums_ref, f32[11,32,256]{2,1,0:T(8,128)S(1)} %get-tuple-element.11.terms_ref, f32[4,32,256]{2,1,0:T(8,128)S(1)} %get-tuple-element.12.basis_ref, f32[3,2,256]{2,1,0:T(2,128)S(1)} %get-tuple-element.13.pic_ref), custom_call_target="tpu_custom_call" | custom-call | tf_op jit(solution)/shard_map/finish/pallas_call | solution.py:1104

commit v7 on v6

--- a/solution.py
+++ b/solution.py
@@ -602,7 +602,7 @@
 OWNED = 32
 MSG = 24
 TRIPLE = 3
-LAG = 3
+LAG = 4
 GIVEN = 9 * PAIR
 
 
@@ -751,7 +751,7 @@
         )
 
     def back(i, part):
-        at, size = ((0, 16), (16, 8))[part]
+        at, size = ((0, 6 * PAIR), (16, 8))[part]
         return pltpu.make_async_remote_copy(
             src_ref=answer.at[:, pl.ds(pl.multiple_of(i * MSG + at, 8), size)], dst_ref=held.at[i, :, pl.ds(at, size)],
             send_sem=back_sems.at[0, part, i], recv_sem=back_sems.at[1, part, i],
@@ -814,7 +814,7 @@
             scatter(answer, at[k], MSG, found[k * STEPS : (k + 1) * STEPS])
 
     for r in range(6):
-        pick_row(coef[r], (r, 8 + r))
+        pick_row(coef[r], (r, 6 + r))
     each(lambda i: back(i, 0).start())
     held[0, :, 0:16] = answer[:, 0:16, :]
 
@@ -833,8 +833,10 @@
 
     def powers_of(i):
         powers = []
+        both = jnp.concatenate([tile_of(held, i, 0), tile_of(held, i, 8)], axis=0)
         for k in range(PAIR):
-            high, mid, low = [p.astype(f32) for p in split3(tile_of(held, i, 8 * k))]
+            rows = jnp.concatenate([both[6 * k : 6 * k + 6], jnp.zeros((2, BLOCK), f32)], axis=0)
+            high, mid, low = [p.astype(f32) for p in split3(rows)]
             coefs = jnp.concatenate([high, mid, low, jnp.zeros_like(low)], axis=0).astype(bf16)
             powers.append(dot(mono_cols, coefs))
         return powers
@@ -971,7 +973,7 @@
         sum_pair(i)
         slope_pair(after, columns, tints)
         turn(far(n + 2))
-        for d in range(4):
+        for d in (2, 1, 3, 0):
             give(i, d).start()
         return 0
 

time: 30.5 us -> 29.8 us (0.977)
  Pallas kernels: 29.7 us -> 29.1 us
    pallas_call x1, Pallas kernels: 28.5 us -> 27.8 us  [fused(): pl.pallas_call(functools.partial(fused_kernel, bands), name='splat', out_...]
where the time goes in v7:
time: 29.8 us; the launch traced here: 29.7 us
  Pallas kernels  29.1 us (98%)
  between operations  0.64 us (2%)
    pallas_call x1, Pallas kernels, fused(): pl.pallas_call(functools.partial(fused_kernel, bands), name='splat', out_...  27.8 us
    pallas_call x1, Pallas kernels, finish(): pl.pallas_call(functools.partial(finish_kernel, bands), name='finish', ou...  1.21 us

profile of v7, /device:TPU:0, one launch (start us, length us, event | category | flops | bytes accessed | tf_op | source)
XLA Modules:
  0.0 29.7 jit_solution(7327576202978790421)
XLA Ops:
  0.6 27.8 %splat.1 = (f32[3,2,256]{2,1,0:T(2,128)S(1)}, f32[4,32,256]{2,1,0:T(8,128)S(1)}, f32[11,32,256]{2,1,0:T(8,128)S(1)}, f32[2,288,128]{2,1,0:T(8,128)S(1)}) custom-call(f32[6,8192]{1,0:T(8,128)} %geometry_hbm.1, f32[2,8192]{1,0:T(2,128)} %angles_hbm.1, f32[12,8192]{1,0:T(8,128)} %coeffs_hbm.1, s32[2,16]{1,0:T(2,128)} %visible_hbm.1, s32[2,16]{1,0:T(2,128)} %order_hbm.1, ...), custom_call_target="tpu_custom_call" | custom-call | tf_op jit(solution)/shard_map/splat/pallas_call | solution.py:1040
  28.5 1.2 %finish.1 = (f32[6,8192]{1,0:T(8,128)}, f32[12,8192]{1,0:T(8,128)}, f32[3,2,256]{2,1,0:T(2,128)}) custom-call(f32[2,288,128]{2,1,0:T(8,128)S(1)} %get-tuple-element.10.sums_ref, f32[11,32,256]{2,1,0:T(8,128)S(1)} %get-tuple-element.11.terms_ref, f32[4,32,256]{2,1,0:T(8,128)S(1)} %get-tuple-element.12.basis_ref, f32[3,2,256]{2,1,0:T(2,128)S(1)} %get-tuple-element.13.pic_ref), custom_call_target="tpu_custom_call" | custom-call | tf_op jit(solution)/shard_map/finish/pallas_call | solution.py:1106

commit v8 on v7

--- a/solution.py
+++ b/solution.py
@@ -971,10 +971,10 @@
         columns = columns_ref[...]
         tints = tints_of(after, columns)
         sum_pair(i)
+        for d in (2, 1, 3, 0):
+            give(i, d).start()
         slope_pair(after, columns, tints)
         turn(far(n + 2))
-        for d in (2, 1, 3, 0):
-            give(i, d).start()
         return 0
 
     turn(far(1))

time: 29.8 us -> 29.7 us (level)
  no operation moved by 1% of the time
where the time goes in v8:
time: 29.7 us; the launch traced here: 29.6 us
  Pallas kernels  28.9 us (97%)
  between operations  0.64 us (2%)
    pallas_call x1, Pallas kernels, fused(): pl.pallas_call(functools.partial(fused_kernel, bands), name='splat', out_...  27.7 us
    pallas_call x1, Pallas kernels, finish(): pl.pallas_call(functools.partial(finish_kernel, bands), name='finish', ou...  1.21 us

profile of v8, /device:TPU:0, one launch (start us, length us, event | category | flops | bytes accessed | tf_op | source)
XLA Modules:
  0.0 29.6 jit_solution(4163208058361069752)
XLA Ops:
  0.6 27.7 %splat.1 = (f32[3,2,256]{2,1,0:T(2,128)S(1)}, f32[4,32,256]{2,1,0:T(8,128)S(1)}, f32[11,32,256]{2,1,0:T(8,128)S(1)}, f32[2,288,128]{2,1,0:T(8,128)S(1)}) custom-call(f32[6,8192]{1,0:T(8,128)} %geometry_hbm.1, f32[2,8192]{1,0:T(2,128)} %angles_hbm.1, f32[12,8192]{1,0:T(8,128)} %coeffs_hbm.1, s32[2,16]{1,0:T(2,128)} %visible_hbm.1, s32[2,16]{1,0:T(2,128)} %order_hbm.1, ...), custom_call_target="tpu_custom_call" | custom-call | tf_op jit(solution)/shard_map/splat/pallas_call | solution.py:1040
  28.4 1.2 %finish.1 = (f32[6,8192]{1,0:T(8,128)}, f32[12,8192]{1,0:T(8,128)}, f32[3,2,256]{2,1,0:T(2,128)}) custom-call(f32[2,288,128]{2,1,0:T(8,128)S(1)} %get-tuple-element.10.sums_ref, f32[11,32,256]{2,1,0:T(8,128)S(1)} %get-tuple-element.11.terms_ref, f32[4,32,256]{2,1,0:T(8,128)S(1)} %get-tuple-element.12.basis_ref, f32[3,2,256]{2,1,0:T(2,128)S(1)} %get-tuple-element.13.pic_ref), custom_call_target="tpu_custom_call" | custom-call | tf_op jit(solution)/shard_map/finish/pallas_call | solution.py:1106
